TPU v7x, 32 devices: a whole 2x2x4 slice. The times are simulated.
32 devices in a mesh: group: 4 (over y, core), dev: 8 (over z, x).
Axes of the slice: x: 2, y: 2, z: 4, core: 2. Of those that a mesh axis runs over, the one named last changes fastest.
Arguments:
- schur: float32 [32, 1024, 1024], P(('group', 'dev'))
- coarse_modes: float32 [32, 6, 512], P(('group', 'dev')), may hold values from -4 to 4
- load: float32 [32, 64, 512], P(('group', 'dev')), may hold values from -6 to 6
- warm_start: float32 [32, 64, 512], P(('group', 'dev')), may hold values from -0.6 to 0.6
- active_blocks: int32 [32], P(('group', 'dev')), may hold values from 1 to 4, as said below
- contact_from: int32 [32], P(('group', 'dev')), may hold values from 0 to 127
Outputs:
- multipliers: float32 [32, 64, 512], P(('group', 'dev'))
- residual: float32 [32, 64, 512], P(('group', 'dev'))
- amplitudes: float32 [64, 6], replicated
Inputs may be any that keep to these rules, and one draw needn't show every extreme that they name: Interface s carries multipliers on its first active_blocks[s] * 128 dofs only; some interface has 1 block and some has all.
All inputs are finite; a program needn't handle non-finite values.
Results may differ from a plain program's by a relative error of at most 0.00023.
Values sent between devices are 32-bit elements; how exact they have to be, the bound alone decides.
No kernel may reach another device: no remote copies, remote signals or barrier semaphores. Data moves between devices by JAX's collectives and lax.ppermute only.
A program may use at most 64 MiB of HBM per device.

v0:
```python
import functools
import math

import jax
import jax.numpy as jnp
from jax import lax
from jax.experimental import pallas as pl
from jax.experimental.pallas import tpu as pltpu
from jax.sharding import PartitionSpec as P

BLK = 128
ITERS = 3
LOWER = 0.1
UPPER = 8.0
THETA = (LOWER + UPPER) / 2.0
DELTA = (UPPER - LOWER) / 2.0
SIGMA = THETA / DELTA

AXES = ("group", "dev")
LANES = 128
ROWS = 8
CHUNK = 128
F32 = jnp.float32
BF16 = jnp.bfloat16
HIGHEST = lax.Precision.HIGHEST
VMEM = pl.BlockSpec(memory_space=pltpu.VMEM)
SMEM = pl.BlockSpec(memory_space=pltpu.SMEM)
ANY = pl.BlockSpec(memory_space=pl.ANY)


def split(x):
    high = x.astype(BF16)
    return high, (x - high.astype(F32)).astype(BF16)


def dot(a, b):
    return jnp.dot(a, b, preferred_element_type=F32)


def product(x, high, low):
    cases = x.shape[0]
    x_high, x_low = split(x)
    both = dot(jnp.concatenate([x_high, x_low], axis=0), high)
    return both[:cases] + (both[cases:] + dot(x_high, low))


def position():
    me = lax.axis_index("group") * lax.axis_size("dev") + lax.axis_index("dev")
    return me, lax.axis_size("group") * lax.axis_size("dev")


def pack_kernel(count_ref, from_ref, warm_ref, modes_ref, out_ref):
    cases, width = warm_ref.shape
    terms = modes_ref.shape[0]
    dofs = lax.broadcasted_iota(jnp.int32, (1, width), 1)
    alive = dofs < count_ref[0] * BLK
    live = alive.astype(F32)
    contact = (alive & (dofs >= from_ref[0])).astype(F32)
    out_ref[:cases, :] = warm_ref[...] * live
    out_ref[cases:, :] = jnp.zeros((2 * ROWS, width), F32)
    out_ref[cases : cases + terms, :] = modes_ref[...] * live
    out_ref[cases + ROWS : cases + ROWS + 1, :] = live
    out_ref[cases + ROWS + 1 : cases + ROWS + 2, :] = contact


def first_kernel(terms, schur_ref, msg_ref, high_ref, low_ref, own_ref, gram_ref, raw, acc, wide, sems):
    order = schur_ref.shape[0]
    cases = own_ref.shape[0]
    chunks = order // CHUNK
    half = chunks // 2
    sequence = list(range(half, chunks)) + list(range(half))

    def copy(c):
        rows = pl.ds(c * CHUNK, CHUNK)
        return pltpu.make_async_copy(schur_ref.at[rows, :], raw.at[rows, :], sems.at[c])

    for c in sequence:
        copy(c).start()
    modes = msg_ref[cases : cases + ROWS, :]
    wide[...] = jnp.zeros_like(wide)
    wide[:, :ROWS] = lax.dot_general(
        modes, modes, (((1,), (1,)), ((), ())), precision=HIGHEST, preferred_element_type=F32
    )
    row = wide[0:1, :]
    for c in range(1, terms):
        row = row + pltpu.roll(wide[c : c + 1, :], ROWS * c, 1)
    gram_ref[...] = row
    for n, c in enumerate(sequence):
        copy(c).wait()
        rows = pl.ds(c * CHUNK, CHUNK)
        high, low = split(raw[rows, :])
        high_ref[rows, :] = high
        low_ref[rows, :] = low
        if n < half:
            part = product(msg_ref[:cases, n * CHUNK : (n + 1) * CHUNK], high, low)
            if n == 0:
                acc[...] = part
            else:
                acc[...] += part
    own_ref[...] = acc[...]


def send(even, left_half, right_half, near_ref, far_ref):
    near_ref[...] = jnp.where(even, right_half, left_half)
    far_ref[...] = jnp.where(even, left_half, right_half)


def pay(terms, modes2, z2, gram_row, pay_ref):
    cases = z2.shape[0]
    per_row = LANES // cases
    coef = lax.dot_general(
        modes2, z2, (((1,), (1,)), ((), ())), precision=HIGHEST, preferred_element_type=F32
    )
    used = terms // per_row
    parts = [coef[p * used : (p + 1) * used, :] for p in range(per_row)]
    block = jnp.concatenate(parts, axis=1)
    slots = pay_ref.shape[0]
    pay_ref[:, :used, :] = jnp.broadcast_to(block[None], (slots, used, LANES))
    pay_ref[:, used : used + 1, :] = jnp.broadcast_to(gram_row[None], (slots, 1, LANES))


def second_kernel(
    terms, high_ref, low_ref, own_ref, halo_ref, msg_ref, load_ref, gram_ref,
    near_ref, far_ref, pay_ref, mult_ref, side_ref,
):
    cases, width = load_ref.shape
    me, _ = position()
    halo = jnp.where(me > 0, halo_ref[...], 0.0)
    left = halo[:cases]
    y = own_ref[...] - product(left, high_ref[:width, :], low_ref[:width, :])
    y_left = y[:, :width]
    rest = load_ref[...] - y[:, width:]
    side = jnp.concatenate([halo[cases:], msg_ref[cases:, :]], axis=1)
    send(me % 2 == 0, y_left, rest, near_ref, far_ref)
    pay(terms, side[:ROWS], jnp.concatenate([y_left, rest], axis=1), gram_ref[...], pay_ref)
    mult_ref[...] = jnp.concatenate([left, msg_ref[:cases, :]], axis=1)
    side_ref[...] = side


def factor_rows(row, terms):
    def entry(c, e):
        lane = ROWS * c + e
        return jnp.broadcast_to(row[:, lane : lane + 1], (1, LANES))

    lower = {}
    inverse = []
    for j in range(terms):
        pivot = entry(j, j)
        for k in range(j):
            pivot = pivot - lower[j, k] * lower[j, k]
        root = jnp.sqrt(pivot)
        inverse.append(1.0 / root)
        for i in range(j + 1, terms):
            value = entry(i, j)
            for k in range(j):
                value = value - lower[i, k] * lower[j, k]
            lower[i, j] = value * inverse[j]
    return lower, inverse


def store_factor(lower, inverse, fac_ref):
    terms = len(inverse)
    n = 0
    for j in range(terms):
        fac_ref[n : n + 1, :] = inverse[j]
        n += 1
    for j in range(terms):
        for i in range(j + 1, terms):
            fac_ref[n : n + 1, :] = lower[i, j]
            n += 1


def load_factor(terms, fac_ref):
    inverse = [fac_ref[j : j + 1, :] for j in range(terms)]
    lower = {}
    n = terms
    for j in range(terms):
        for i in range(j + 1, terms):
            lower[i, j] = fac_ref[n : n + 1, :]
            n += 1
    return lower, inverse


def solve(total, lower, inverse, cases, amp_ref):
    terms = len(inverse)
    per_row = LANES // cases
    used = terms // per_row
    known = []
    for c in range(terms):
        row = total[c % used : c % used + 1, :]
        value = row if c < used else pltpu.roll(row, LANES - (c // used) * cases, 1)
        for k in range(c):
            value = value - lower[c, k] * known[k]
        known.append(value * inverse[c])
    for c in reversed(range(terms)):
        value = known[c]
        for k in range(c + 1, terms):
            value = value - lower[k, c] * known[k]
        known[c] = value * inverse[c]
    amp_ref[...] = jnp.zeros_like(amp_ref)
    for c in range(terms):
        amp_ref[c : c + 1, :] = known[c]
    return amp_ref[...][:, :cases]


def chebyshev(residual, update, rhos):
    rho, rho_new = rhos
    if rho is None:
        return residual / THETA
    return rho_new * rho * update + 2.0 * rho_new / DELTA * residual


def project(amp, modes):
    return lax.dot_general(
        amp, modes, (((0,), (0,)), ((), ())), precision=HIGHEST, preferred_element_type=F32
    )


def middle_kernel(
    terms, first, rhos, sum_ref, near_ref, far_ref, near_in, far_in, mult_ref, side_ref, load_ref,
    high_ref, low_ref, *rest,
):
    if first:
        near_out, far_out, pay_ref, mult_out, upd_out, fac_out, amp_ref = rest
    else:
        upd_ref, fac_ref, near_out, far_out, pay_ref, mult_out, upd_out, amp_ref = rest
    cases, width = load_ref.shape
    me, devices = position()
    even = me % 2 == 0
    total = jnp.sum(sum_ref[...], axis=0)
    if first:
        used = total.shape[0] - 1
        lower, inverse = factor_rows(total[used : used + 1, :], terms)
        store_factor(lower, inverse, fac_out)
    else:
        lower, inverse = load_factor(terms, fac_ref)
    amp = solve(total, lower, inverse, cases, amp_ref)
    near = near_ref[...] + near_in[...]
    far = far_ref[...] + jnp.where((me == devices - 1), 0.0, far_in[...])
    live = side_ref[ROWS : ROWS + 1, :]
    contact = side_ref[ROWS + 1 : ROWS + 2, :] > 0.0
    modes = side_ref[:ROWS, :]
    open_part = jnp.concatenate([jnp.where(even, far, near), jnp.where(even, near, far)], axis=1)
    open_part = jnp.where(live > 0.0, open_part, 0.0)
    residual = open_part - project(amp, modes)
    update = chebyshev(residual, None if first else upd_ref[...], rhos)
    mult = mult_ref[...] + update
    mult = jnp.where(contact, jnp.maximum(mult, 0.0), mult)
    mult_out[...] = mult
    upd_out[...] = update
    y = product(jnp.concatenate([-mult[:, :width], mult[:, width:]], axis=1), high_ref[...], low_ref[...])
    y_left = y[:, :width]
    rest_part = load_ref[...] - y[:, width:]
    send(even, y_left, rest_part, near_out, far_out)
    pay(terms, modes, jnp.concatenate([y_left, rest_part], axis=1), jnp.zeros((1, LANES), F32), pay_ref)


def last_kernel(
    terms, rhos, sum_ref, near_ref, far_ref, near_in, far_in, mult_ref, side_ref, upd_ref, fac_ref,
    mult_out, res_out, amp_out, amp_ref,
):
    cases, width = mult_out.shape
    me, devices = position()
    even = me % 2 == 0
    total = jnp.sum(sum_ref[...], axis=0)
    lower, inverse = load_factor(terms, fac_ref)
    amp = solve(total, lower, inverse, cases, amp_ref)
    near = near_ref[...] + near_in[...]
    far = far_ref[...] + jnp.where((me == devices - 1), 0.0, far_in[...])
    live = side_ref[ROWS : ROWS + 1, width:]
    contact = side_ref[ROWS + 1 : ROWS + 2, width:] > 0.0
    open_part = jnp.where(live > 0.0, jnp.where(even, near, far), 0.0)
    residual = open_part - project(amp, side_ref[:ROWS, width:])
    update = chebyshev(residual, upd_ref[:, width:], rhos)
    mult = mult_ref[:, width:] + update
    mult_out[...] = jnp.where(contact, jnp.maximum(mult, 0.0), mult)
    res_out[...] = residual
    amp_out[...] = jnp.transpose(amp_ref[...])[:cases, :terms]


def shaped(*shapes):
    return [jax.ShapeDtypeStruct(s, d) for s, d in shapes]


def params(megabytes):
    return pltpu.CompilerParams(vmem_limit_bytes=megabytes << 20)


def shards(schur, coarse_modes, load, warm_start, active_blocks, contact_from):
    _, cases, width = load.shape
    order = schur.shape[1]
    terms = coarse_modes.shape[1]
    devices = lax.axis_size("group") * lax.axis_size("dev")
    slot = terms // (LANES // cases) + 1
    ring = [(i, (i + 1) % devices) for i in range(devices)]
    near_pairs = [(i, i ^ 1) for i in range(devices)]
    far_pairs = [(i, (i + (1 if i % 2 else devices - 1)) % devices) for i in range(devices)]

    rhos = [(None, None)]
    rho = 1.0 / SIGMA
    for _ in range(1, ITERS):
        rho_new = 1.0 / (2.0 * SIGMA - rho)
        rhos.append((rho, rho_new))
        rho = rho_new

    msg = pl.pallas_call(
        pack_kernel,
        out_shape=jax.ShapeDtypeStruct((cases + 2 * ROWS, width), F32),
        in_specs=[SMEM, SMEM, VMEM, VMEM],
        out_specs=VMEM,
        compiler_params=params(4),
        name="pack",
    )(active_blocks, contact_from, warm_start[0], coarse_modes[0])
    halo = lax.ppermute(msg, AXES, ring)
    high, low, own, gram_row = pl.pallas_call(
        functools.partial(first_kernel, terms),
        out_shape=shaped(
            ((order, order), BF16), ((order, order), BF16), ((cases, order), F32), ((1, LANES), F32)
        ),
        in_specs=[ANY, VMEM],
        out_specs=[VMEM] * 4,
        scratch_shapes=[
            pltpu.VMEM((order, order), F32),
            pltpu.VMEM((cases, order), F32),
            pltpu.VMEM((ROWS, LANES), F32),
            pltpu.SemaphoreType.DMA((order // CHUNK,)),
        ],
        compiler_params=params(16),
        cost_estimate=pl.CostEstimate(
            flops=4 * cases * order * order, bytes_accessed=8 * order * order, transcendentals=0
        ),
        name="first",
    )(schur[0], msg)

    half = ((cases, width), F32)
    full = ((cases, order), F32)
    payload = ((devices, slot, LANES), F32)
    rows = ((math.ceil(terms * (terms + 1) // 2 / ROWS) * ROWS, LANES), F32)
    near, far, pay_out, mult, side = pl.pallas_call(
        functools.partial(second_kernel, terms),
        out_shape=shaped(half, half, payload, full, ((2 * ROWS, order), F32)),
        in_specs=[VMEM] * 7,
        out_specs=[VMEM] * 5,
        compiler_params=params(8),
        name="second",
    )(high, low, own, halo, msg, load[0], gram_row)

    update = factor = None
    amp_scratch = [pltpu.VMEM((ROWS, LANES), F32)]
    for step in range(ITERS):
        far_in = lax.ppermute(far, AXES, far_pairs)
        near_in = lax.ppermute(near, AXES, near_pairs)
        gathered = lax.all_to_all(pay_out, AXES, 0, 0)
        first = step == 0
        if step < ITERS - 1:
            inputs = [gathered, near, far, near_in, far_in, mult, side, load[0], high, low]
            outputs = [half, half, payload, full, full]
            if first:
                outputs.append(rows)
            else:
                inputs += [update, factor]
            out = pl.pallas_call(
                functools.partial(middle_kernel, terms, first, rhos[step]),
                out_shape=shaped(*outputs),
                in_specs=[VMEM] * len(inputs),
                out_specs=[VMEM] * len(outputs),
                scratch_shapes=amp_scratch,
                compiler_params=params(12),
            )(*inputs)
            near, far, pay_out, mult, update = out[:5]
            if first:
                factor = out[5]
        else:
            inputs = [gathered, near, far, near_in, far_in, mult, side, update, factor]
            mult, residual, amplitudes = pl.pallas_call(
                functools.partial(last_kernel, terms, rhos[step]),
                out_shape=shaped(half, half, ((cases, terms), F32)),
                in_specs=[VMEM] * len(inputs),
                out_specs=[VMEM] * 3,
                scratch_shapes=amp_scratch,
                compiler_params=params(8),
                name="last",
            )(*inputs)
    return mult[None], residual[None], amplitudes


def solution(mesh):
    placed = (
        P(AXES, None, None),
        P(AXES, None, None),
        P(AXES, None, None),
        P(AXES, None, None),
        P(AXES),
        P(AXES),
    )
    return jax.shard_map(
        shards,
        mesh=mesh,
        in_specs=placed,
        out_specs=(P(AXES, None, None), P(AXES, None, None), P()),
        check_vma=False,
    )
```

profile of v0, /device:TPU:0, one launch (start us, length us, event | category | flops | bytes accessed | tf_op | source)
XLA Modules:
  0.0 61.5 jit_solution(12268973321105639733)
XLA Ops:
  1.9 0.7 %copy.12 = f32[1,6,512]{2,1,0:T(8,128)S(1)} copy(f32[1,6,512]{2,0,1:T(1,128)} %param.7) | data formatting | bytes 24576
  2.6 0.0 copy-start.2
  2.6 0.9 %copy-done.2 = f32[1,64,512]{2,1,0:T(8,128)S(1)} copy-done((f32[1,64,512]{2,1,0:T(8,128)S(1)}, f32[1,64,512]{2,1,0:T(8,128)}, u32[]{:S(2)}) %copy-start.2) | copy-done | bytes 131096
  3.6 3.0 %collective-permute-start = (f32[80,512]{1,0:T(8,128)S(1)}, f32[80,512]{1,0:T(8,128)S(1)}, u32[]{:S(2)}, u32[]{:S(2)}) collective-permute-start(f32[80,512]{1,0:T(8,128)S(1)} %pack.1.msg_ref), channel_id=1, source_target_pairs={{0,1},{1,2},{2,3},{3,4},{4,5},{5,6},{6,7},{7,8},{8,9},{9,10},{10,1... | collective-permute-start | bytes 491528 | tf_op jit(solution)/shard_map/ppermute | solution.py:314
  6.6 0.0 copy-start
  6.6 2.2 %copy-done = f32[1,1024,1024]{2,1,0:T(8,128)S(1)} copy-done((f32[1,1024,1024]{2,1,0:T(8,128)S(1)}, f32[1,1024,1024]{2,1,0:T(8,128)}, u32[]{:S(2)}) %copy-start) | copy-done | bytes 4194328
  8.8 0.0 copy-start.1
  8.8 1.9 %first.1 = (bf16[1024,1024]{1,0:T(8,128)(2,1)S(1)}, bf16[1024,1024]{1,0:T(8,128)(2,1)S(1)}, f32[64,1024]{1,0:T(8,128)S(1)}, f32[1,128]{1,0:T(1,128)S(1)}) custom-call(f32[1024,1024]{1,0:T(8,128)S(1)} %bitcast.8, f32[80,512]{1,0:T(8,128)S(1)} %pack.1.msg_ref), custom_call_target="tpu_custom_call" | custom-call | flops 268435456 | bytes 8388608 | tf_op jit(solution)/shard_map/first/pallas_call | solution.py:315
  10.6 3.3 %collective-permute-done.halo_ref = f32[80,512]{1,0:T(8,128)S(1)} collective-permute-done((f32[80,512]{1,0:T(8,128)S(1)}, f32[80,512]{1,0:T(8,128)S(1)}, u32[]{:S(2)}, u32[]{:S(2)}) %collective-permute-start) | collective-permute-done | bytes 163872 | tf_op jit(solution)/shard_map/ppermute | solution.py:314
  13.9 0.0 copy-done.1
  13.9 1.1 %second.1 = (f32[64,512]{1,0:T(8,128)S(1)}, f32[64,512]{1,0:T(8,128)S(1)}, f32[32,4,128]{2,1,0:T(4,128)S(1)}, f32[64,1024]{1,0:T(8,128)S(1)}, f32[16,1024]{1,0:T(8,128)S(1)}) custom-call(bf16[1024,1024]{1,0:T(8,128)(2,1)S(1)} %get-tuple-element.26.high_ref, bf16[1024,1024]{1,0:T(8,128)(2,1)S(1)} %get-tuple-element.27.low_ref, ...), custom_call_target="tpu_custom_call" | custom-call | tf_op jit(solution)/shard_map/second/pallas_call | solution.py:339
  15.0 0.1 collective-permute-start.1
  15.1 2.3 %collective-permute-start.2 = (f32[64,512]{1,0:T(8,128)S(1)}, f32[64,512]{1,0:T(8,128)S(1)}, u32[]{:S(2)}, u32[]{:S(2)}) collective-permute-start(f32[64,512]{1,0:T(8,128)S(1)} %get-tuple-element.32.far_ref), channel_id=1, source_target_pairs={{0,31},{1,2},{2,1},{3,4},{4,3},{5,6},{6,5},{7,8},{8,7},{9,10},{10,... | collective-permute-start | bytes 393224 | tf_op jit(solution)/shard_map/ppermute | solution.py:351
  17.4 11.3 %all_to_all.15.sum_ref = f32[32,4,128]{2,1,0:T(4,128)S(1)} all-to-all(f32[32,4,128]{2,1,0:T(4,128)S(1)} %get-tuple-element.30), channel_id=1, replica_groups=mesh['group'=4,'dev'=8] {'group','dev'}, dimensions={0} | all-to-all | bytes 131072 | tf_op jit(solution)/shard_map/all_to_all | solution.py:353
  28.7 0.0 collective-permute-done.1.near_in
  28.7 0.0 collective-permute-done.2.far_in
  28.7 1.9 %shard_map.85 = (f32[64,512]{1,0:T(8,128)S(1)}, f32[64,512]{1,0:T(8,128)S(1)}, f32[32,4,128]{2,1,0:T(4,128)S(1)}, f32[64,1024]{1,0:T(8,128)S(1)}, f32[64,1024]{1,0:T(8,128)S(1)}, /*index=5*/f32[24,128]{1,0:T(8,128)S(1)}) custom-call(f32[32,4,128]{2,1,0:T(4,128)S(1)} %all_to_all.15.sum_ref, f32[64,512]{1,0:T(8,128)S(1)} %get-tuple-element.31.near_ref, ...), custom_call_target="tpu_custom_call" | custom-call | tf_op jit(solution)/shard_map/pallas_call | solution.py:362
  30.6 0.8 %collective-permute-start.3 = (f32[64,512]{1,0:T(8,128)S(1)}, f32[64,512]{1,0:T(8,128)S(1)}, u32[]{:S(2)}, u32[]{:S(2)}) collective-permute-start(f32[64,512]{1,0:T(8,128)S(1)} %get-tuple-element.36.near_ref), channel_id=1, source_target_pairs={{0,1},{1,0},{2,3},{3,2},{4,5},{5,4},{6,7},{7,6},{8,9},{9,8},{10,11... | collective-permute-start | bytes 393224 | tf_op jit(solution)/shard_map/ppermute | solution.py:352
  31.4 0.9 %collective-permute-start.4 = (f32[64,512]{1,0:T(8,128)S(1)}, f32[64,512]{1,0:T(8,128)S(1)}, u32[]{:S(2)}, u32[]{:S(2)}) collective-permute-start(f32[64,512]{1,0:T(8,128)S(1)} %get-tuple-element.37.far_ref), channel_id=1, source_target_pairs={{0,31},{1,2},{2,1},{3,4},{4,3},{5,6},{6,5},{7,8},{8,7},{9,10},{10,... | collective-permute-start | bytes 393224 | tf_op jit(solution)/shard_map/ppermute | solution.py:351
  32.3 11.9 %all_to_all.16.sum_ref = f32[32,4,128]{2,1,0:T(4,128)S(1)} all-to-all(f32[32,4,128]{2,1,0:T(4,128)S(1)} %get-tuple-element.35), channel_id=1, replica_groups=mesh['group'=4,'dev'=8] {'group','dev'}, dimensions={0} | all-to-all | bytes 131072 | tf_op jit(solution)/shard_map/all_to_all | solution.py:353
  44.2 0.0 collective-permute-done.3.near_in
  44.2 0.0 collective-permute-done.4.far_in
  44.2 1.8 %shard_map.86 = (f32[64,512]{1,0:T(8,128)S(1)}, f32[64,512]{1,0:T(8,128)S(1)}, f32[32,4,128]{2,1,0:T(4,128)S(1)}, f32[64,1024]{1,0:T(8,128)S(1)}, f32[64,1024]{1,0:T(8,128)S(1)}) custom-call(f32[32,4,128]{2,1,0:T(4,128)S(1)} %all_to_all.16.sum_ref, f32[64,512]{1,0:T(8,128)S(1)} %get-tuple-element.36.near_ref, f32[64,512]{1,0:T(8,128)S(1)} %get-tuple-element.37.far_ref, ...), custom_call_target="tpu_custom_call" | custom-call | tf_op jit(solution)/shard_map/pallas_call | solution.py:362
  46.0 0.8 %collective-permute-start.5 = (f32[64,512]{1,0:T(8,128)S(1)}, f32[64,512]{1,0:T(8,128)S(1)}, u32[]{:S(2)}, u32[]{:S(2)}) collective-permute-start(f32[64,512]{1,0:T(8,128)S(1)} %get-tuple-element.42.near_ref), channel_id=1, source_target_pairs={{0,1},{1,0},{2,3},{3,2},{4,5},{5,4},{6,7},{7,6},{8,9},{9,8},{10,11... | collective-permute-start | bytes 393224 | tf_op jit(solution)/shard_map/ppermute | solution.py:352
  46.9 0.9 %collective-permute-start.6 = (f32[64,512]{1,0:T(8,128)S(1)}, f32[64,512]{1,0:T(8,128)S(1)}, u32[]{:S(2)}, u32[]{:S(2)}) collective-permute-start(f32[64,512]{1,0:T(8,128)S(1)} %get-tuple-element.43.far_ref), channel_id=1, source_target_pairs={{0,31},{1,2},{2,1},{3,4},{4,3},{5,6},{6,5},{7,8},{8,7},{9,10},{10,... | collective-permute-start | bytes 393224 | tf_op jit(solution)/shard_map/ppermute | solution.py:351
  47.8 11.9 %all_to_all.17.sum_ref = f32[32,4,128]{2,1,0:T(4,128)S(1)} all-to-all(f32[32,4,128]{2,1,0:T(4,128)S(1)} %get-tuple-element.41), channel_id=1, replica_groups=mesh['group'=4,'dev'=8] {'group','dev'}, dimensions={0} | all-to-all | bytes 131072 | tf_op jit(solution)/shard_map/all_to_all | solution.py:353
  59.7 0.0 collective-permute-done.5.near_in
  59.7 0.0 collective-permute-done.6.far_in
  59.7 1.2 %last.1 = (f32[64,512]{1,0:T(8,128)}, f32[64,512]{1,0:T(8,128)}, f32[64,6]{1,0:T(8,128)S(1)}) custom-call(f32[32,4,128]{2,1,0:T(4,128)S(1)} %all_to_all.17.sum_ref, f32[64,512]{1,0:T(8,128)S(1)} %get-tuple-element.42.near_ref, f32[64,512]{1,0:T(8,128)S(1)} %get-tuple-element.43.far_ref, f32[64,512]{1,0:T(8,128)S(1)} %collective-permute-done.5.near_in, ...), custom_call_target="tpu_custom_call" | custom-call | tf_op jit(solution)/shard_map/last/pallas_call | solution.py:375
  60.8 0.7 %copy.9 = f32[64,6]{0,1:T(8,128)} copy(f32[64,6]{1,0:T(8,128)S(1)} %get-tuple-element.51) | data formatting | bytes 3072
  (1 shorter events, 0.0 us)
Async XLA Ops:
  2.6 0.9 %copy-start.2 = (f32[1,64,512]{2,1,0:T(8,128)S(1)}, f32[1,64,512]{2,1,0:T(8,128)}, u32[]{:S(2)}) copy-start(f32[1,64,512]{2,1,0:T(8,128)} %param.9) | copy-start | bytes 393220
  3.6 10.4 %collective-permute-start = (f32[80,512]{1,0:T(8,128)S(1)}, f32[80,512]{1,0:T(8,128)S(1)}, u32[]{:S(2)}, u32[]{:S(2)}) collective-permute-start(f32[80,512]{1,0:T(8,128)S(1)} %pack.1.msg_ref), channel_id=1, source_target_pairs={{0,1},{1,2},{2,3},{3,4},{4,5},{5,6},{6,7},{7,8},{8,9},{9,10},{10,1... | collective-permute-start | bytes 491528 | tf_op jit(solution)/shard_map/ppermute | solution.py:314
  6.6 2.2 %copy-start = (f32[1,1024,1024]{2,1,0:T(8,128)S(1)}, f32[1,1024,1024]{2,1,0:T(8,128)}, u32[]{:S(2)}) copy-start(f32[1,1024,1024]{2,1,0:T(8,128)} %param.6) | copy-start | bytes 12582916
  8.8 5.1 %copy-start.1 = (f32[1,64,512]{2,1,0:T(8,128)S(1)}, f32[1,64,512]{2,1,0:T(8,128)}, u32[]{:S(2)}) copy-start(f32[1,64,512]{2,1,0:T(8,128)} %param.8) | copy-start | bytes 393220
  15.0 13.7 %collective-permute-start.1 = (f32[64,512]{1,0:T(8,128)S(1)}, f32[64,512]{1,0:T(8,128)S(1)}, u32[]{:S(2)}, u32[]{:S(2)}) collective-permute-start(f32[64,512]{1,0:T(8,128)S(1)} %get-tuple-element.31.near_ref), channel_id=1, source_target_pairs={{0,1},{1,0},{2,3},{3,2},{4,5},{5,4},{6,7},{7,6},{8,9},{9,8},{10,11... | collective-permute-start | bytes 393224 | tf_op jit(solution)/shard_map/ppermute | solution.py:352
  15.1 13.6 %collective-permute-start.2 = (f32[64,512]{1,0:T(8,128)S(1)}, f32[64,512]{1,0:T(8,128)S(1)}, u32[]{:S(2)}, u32[]{:S(2)}) collective-permute-start(f32[64,512]{1,0:T(8,128)S(1)} %get-tuple-element.32.far_ref), channel_id=1, source_target_pairs={{0,31},{1,2},{2,1},{3,4},{4,3},{5,6},{6,5},{7,8},{8,7},{9,10},{10,... | collective-permute-start | bytes 393224 | tf_op jit(solution)/shard_map/ppermute | solution.py:351
  30.6 13.6 %collective-permute-start.3 = (f32[64,512]{1,0:T(8,128)S(1)}, f32[64,512]{1,0:T(8,128)S(1)}, u32[]{:S(2)}, u32[]{:S(2)}) collective-permute-start(f32[64,512]{1,0:T(8,128)S(1)} %get-tuple-element.36.near_ref), channel_id=1, source_target_pairs={{0,1},{1,0},{2,3},{3,2},{4,5},{5,4},{6,7},{7,6},{8,9},{9,8},{10,11... | collective-permute-start | bytes 393224 | tf_op jit(solution)/shard_map/ppermute | solution.py:352
  31.4 12.8 %collective-permute-start.4 = (f32[64,512]{1,0:T(8,128)S(1)}, f32[64,512]{1,0:T(8,128)S(1)}, u32[]{:S(2)}, u32[]{:S(2)}) collective-permute-start(f32[64,512]{1,0:T(8,128)S(1)} %get-tuple-element.37.far_ref), channel_id=1, source_target_pairs={{0,31},{1,2},{2,1},{3,4},{4,3},{5,6},{6,5},{7,8},{8,7},{9,10},{10,... | collective-permute-start | bytes 393224 | tf_op jit(solution)/shard_map/ppermute | solution.py:351
  46.0 13.6 %collective-permute-start.5 = (f32[64,512]{1,0:T(8,128)S(1)}, f32[64,512]{1,0:T(8,128)S(1)}, u32[]{:S(2)}, u32[]{:S(2)}) collective-permute-start(f32[64,512]{1,0:T(8,128)S(1)} %get-tuple-element.42.near_ref), channel_id=1, source_target_pairs={{0,1},{1,0},{2,3},{3,2},{4,5},{5,4},{6,7},{7,6},{8,9},{9,8},{10,11... | collective-permute-start | bytes 393224 | tf_op jit(solution)/shard_map/ppermute | solution.py:352
  46.9 12.8 %collective-permute-start.6 = (f32[64,512]{1,0:T(8,128)S(1)}, f32[64,512]{1,0:T(8,128)S(1)}, u32[]{:S(2)}, u32[]{:S(2)}) collective-permute-start(f32[64,512]{1,0:T(8,128)S(1)} %get-tuple-element.43.far_ref), channel_id=1, source_target_pairs={{0,31},{1,2},{2,1},{3,4},{4,3},{5,6},{6,5},{7,8},{8,7},{9,10},{10,... | collective-permute-start | bytes 393224 | tf_op jit(solution)/shard_map/ppermute | solution.py:351
where the time goes:
time: 61.8 us; the launch traced here: 61.5 us
  blocking collectives  35 us (57%)
  starting transfers between devices  8.93 us (14%)
  Pallas kernels  7.79 us (13%)
  local copies, waits for them, and re-layouts  4.47 us (7%)
  waiting for transfers between devices  3.29 us (5%)
  between operations  2.01 us (3%)
    all_to_all x3, blocking collectives, shards(): gathered = lax.all_to_all(pay_out, AXES, 0, 0)  35 us
    unnamed x8, local copies, waits for them, and re-layouts  4.47 us
    ppermute x3, starting transfers between devices, shards(): far_in = lax.ppermute(far, AXES, far_pairs)  4.14 us
    pallas_call x2, Pallas kernels, shards(): pl.pallas_call(functools.partial(middle_kernel, terms, first, rhos[step])...  3.67 us
    ppermute x1, waiting for transfers between devices, shards(): halo = lax.ppermute(msg, AXES, ring)  3.27 us
    ppermute x1, starting transfers between devices, shards(): halo = lax.ppermute(msg, AXES, ring)  3.02 us
    pallas_call x1, Pallas kernels, shards(): pl.pallas_call(functools.partial(first_kernel, terms), out_shape=shaped((...  1.86 us
    ppermute x3, starting transfers between devices, shards(): near_in = lax.ppermute(near, AXES, near_pairs)  1.77 us
  transfers between devices with their start and end apart: 7, of which 1 were waited for; matrix products, arithmetic and copies ran while one was open for 0% of the time, Pallas kernels for 3%

commit v1 on v0

--- a/solution.py
+++ b/solution.py
@@ -33,6 +33,13 @@
     return high, (x - high.astype(F32)).astype(BF16)
 
 
+def split3(x):
+    high = x.astype(BF16)
+    rest = x - high.astype(F32)
+    middle = rest.astype(BF16)
+    return high, middle, (rest - middle.astype(F32)).astype(BF16)
+
+
 def dot(a, b):
     return jnp.dot(a, b, preferred_element_type=F32)
 
@@ -44,6 +51,19 @@
     return both[:cases] + (both[cases:] + dot(x_high, low))
 
 
+def wide_product(x, high_ref, low_ref, start):
+    cases, depth = x.shape
+    x_high, x_low = split(x)
+    both = jnp.concatenate([x_high, x_low], axis=0)
+    out = []
+    for j in range(0, high_ref.shape[0], 2):
+        high = jnp.concatenate([high_ref[j + p, start : start + depth, :] for p in range(2)], axis=1)
+        low = jnp.concatenate([low_ref[j + p, start : start + depth, :] for p in range(2)], axis=1)
+        first = dot(both, high)
+        out.append(first[:cases] + (first[cases:] + dot(x_high, low)))
+    return jnp.concatenate(out, axis=1)
+
+
 def position():
     me = lax.axis_index("group") * lax.axis_size("dev") + lax.axis_index("dev")
     return me, lax.axis_size("group") * lax.axis_size("dev")
@@ -52,15 +72,18 @@
 def pack_kernel(count_ref, from_ref, warm_ref, modes_ref, out_ref):
     cases, width = warm_ref.shape
     terms = modes_ref.shape[0]
+    spare = out_ref.shape[0] - cases - terms
     dofs = lax.broadcasted_iota(jnp.int32, (1, width), 1)
     alive = dofs < count_ref[0] * BLK
     live = alive.astype(F32)
     contact = (alive & (dofs >= from_ref[0])).astype(F32)
     out_ref[:cases, :] = warm_ref[...] * live
-    out_ref[cases:, :] = jnp.zeros((2 * ROWS, width), F32)
-    out_ref[cases : cases + terms, :] = modes_ref[...] * live
-    out_ref[cases + ROWS : cases + ROWS + 1, :] = live
-    out_ref[cases + ROWS + 1 : cases + ROWS + 2, :] = contact
+    for c in range(terms):
+        out_ref[cases + c : cases + c + 1, :] = modes_ref[c] * live
+    if spare > 2:
+        out_ref[cases + terms :, :] = jnp.zeros((spare, width), F32)
+    out_ref[-2:-1, :] = live
+    out_ref[-1:, :] = contact
 
 
 def first_kernel(terms, schur_ref, msg_ref, high_ref, low_ref, own_ref, gram_ref, raw, acc, wide, sems):
@@ -77,6 +100,7 @@
     for c in sequence:
         copy(c).start()
     modes = msg_ref[cases : cases + ROWS, :]
+    modes = jnp.where(lax.broadcasted_iota(jnp.int32, modes.shape, 0) < terms, modes, 0.0)
     wide[...] = jnp.zeros_like(wide)
     wide[:, :ROWS] = lax.dot_general(
         modes, modes, (((1,), (1,)), ((), ())), precision=HIGHEST, preferred_element_type=F32
@@ -89,8 +113,10 @@
         copy(c).wait()
         rows = pl.ds(c * CHUNK, CHUNK)
         high, low = split(raw[rows, :])
-        high_ref[rows, :] = high
-        low_ref[rows, :] = low
+        for j in range(order // LANES):
+            lanes = slice(j * LANES, (j + 1) * LANES)
+            high_ref[j, c * CHUNK : (c + 1) * CHUNK, :] = high[:, lanes]
+            low_ref[j, c * CHUNK : (c + 1) * CHUNK, :] = low[:, lanes]
         if n < half:
             part = product(msg_ref[:cases, n * CHUNK : (n + 1) * CHUNK], high, low)
             if n == 0:
@@ -105,12 +131,14 @@
     far_ref[...] = jnp.where(even, left_half, right_half)
 
 
-def pay(terms, modes2, z2, gram_row, pay_ref):
+def pay(terms, pieces, z2, gram_row, pay_ref):
     cases = z2.shape[0]
     per_row = LANES // cases
-    coef = lax.dot_general(
-        modes2, z2, (((1,), (1,)), ((), ())), precision=HIGHEST, preferred_element_type=F32
-    )
+    across = (((1,), (1,)), ((), ()))
+    z_high, z_low = split(z2)
+    top = lax.dot_general(pieces, z_high, across, preferred_element_type=F32)
+    low = lax.dot_general(pieces, z_low, across, preferred_element_type=F32)
+    coef = top[:ROWS] + ((top[ROWS : 2 * ROWS] + low[:ROWS]) + (top[2 * ROWS : 3 * ROWS] + low[ROWS : 2 * ROWS]))
     used = terms // per_row
     parts = [coef[p * used : (p + 1) * used, :] for p in range(per_row)]
     block = jnp.concatenate(parts, axis=1)
@@ -121,20 +149,24 @@
 
 def second_kernel(
     terms, high_ref, low_ref, own_ref, halo_ref, msg_ref, load_ref, gram_ref,
-    near_ref, far_ref, pay_ref, mult_ref, side_ref,
+    near_ref, far_ref, pay_ref, mult_ref, mask_ref, pieces_ref,
 ):
     cases, width = load_ref.shape
     me, _ = position()
     halo = jnp.where(me > 0, halo_ref[...], 0.0)
     left = halo[:cases]
-    y = own_ref[...] - product(left, high_ref[:width, :], low_ref[:width, :])
+    y = own_ref[...] - wide_product(left, high_ref, low_ref, 0)
     y_left = y[:, :width]
     rest = load_ref[...] - y[:, width:]
-    side = jnp.concatenate([halo[cases:], msg_ref[cases:, :]], axis=1)
+    tail = halo_ref.shape[0] - 2
+    mask_ref[0:2, :] = jnp.concatenate([halo[tail:], msg_ref[tail:, :]], axis=1)
+    modes = jnp.concatenate([halo[cases : cases + ROWS], msg_ref[cases : cases + ROWS, :]], axis=1)
+    modes = jnp.where(lax.broadcasted_iota(jnp.int32, modes.shape, 0) < terms, modes, 0.0)
+    pieces = jnp.concatenate(split3(modes), axis=0)
+    pieces_ref[...] = pieces
     send(me % 2 == 0, y_left, rest, near_ref, far_ref)
-    pay(terms, side[:ROWS], jnp.concatenate([y_left, rest], axis=1), gram_ref[...], pay_ref)
+    pay(terms, pieces, jnp.concatenate([y_left, rest], axis=1), gram_ref[...], pay_ref)
     mult_ref[...] = jnp.concatenate([left, msg_ref[:cases, :]], axis=1)
-    side_ref[...] = side
 
 
 def factor_rows(row, terms):
@@ -200,7 +232,7 @@
     amp_ref[...] = jnp.zeros_like(amp_ref)
     for c in range(terms):
         amp_ref[c : c + 1, :] = known[c]
-    return amp_ref[...][:, :cases]
+    return amp_ref[...]
 
 
 def chebyshev(residual, update, rhos):
@@ -210,14 +242,16 @@
     return rho_new * rho * update + 2.0 * rho_new / DELTA * residual
 
 
-def project(amp, modes):
-    return lax.dot_general(
-        amp, modes, (((0,), (0,)), ((), ())), precision=HIGHEST, preferred_element_type=F32
-    )
+def project(amp, pieces, cases):
+    one, two, three = (p.astype(F32) for p in split3(amp))
+    left = jnp.transpose(jnp.concatenate([one, two, three, one, two, one], axis=0))[:cases]
+    m = [pieces[p * ROWS : (p + 1) * ROWS] for p in range(3)]
+    right = jnp.concatenate([m[0], m[0], m[0], m[1], m[1], m[2]], axis=0)
+    return dot(left.astype(BF16), right)
 
 
 def middle_kernel(
-    terms, first, rhos, sum_ref, near_ref, far_ref, near_in, far_in, mult_ref, side_ref, load_ref,
+    terms, first, rhos, sum_ref, near_ref, far_ref, near_in, far_in, mult_ref, mask_ref, pieces_ref, load_ref,
     high_ref, low_ref, *rest,
 ):
     if first:
@@ -237,26 +271,26 @@
     amp = solve(total, lower, inverse, cases, amp_ref)
     near = near_ref[...] + near_in[...]
     far = far_ref[...] + jnp.where((me == devices - 1), 0.0, far_in[...])
-    live = side_ref[ROWS : ROWS + 1, :]
-    contact = side_ref[ROWS + 1 : ROWS + 2, :] > 0.0
-    modes = side_ref[:ROWS, :]
+    live = mask_ref[0:1, :]
+    contact = mask_ref[1:2, :] > 0.0
+    pieces = pieces_ref[...]
     open_part = jnp.concatenate([jnp.where(even, far, near), jnp.where(even, near, far)], axis=1)
     open_part = jnp.where(live > 0.0, open_part, 0.0)
-    residual = open_part - project(amp, modes)
+    residual = open_part - project(amp, pieces, cases)
     update = chebyshev(residual, None if first else upd_ref[...], rhos)
     mult = mult_ref[...] + update
     mult = jnp.where(contact, jnp.maximum(mult, 0.0), mult)
     mult_out[...] = mult
     upd_out[...] = update
-    y = product(jnp.concatenate([-mult[:, :width], mult[:, width:]], axis=1), high_ref[...], low_ref[...])
+    y = wide_product(jnp.concatenate([-mult[:, :width], mult[:, width:]], axis=1), high_ref, low_ref, 0)
     y_left = y[:, :width]
     rest_part = load_ref[...] - y[:, width:]
     send(even, y_left, rest_part, near_out, far_out)
-    pay(terms, modes, jnp.concatenate([y_left, rest_part], axis=1), jnp.zeros((1, LANES), F32), pay_ref)
+    pay(terms, pieces, jnp.concatenate([y_left, rest_part], axis=1), jnp.zeros((1, LANES), F32), pay_ref)
 
 
 def last_kernel(
-    terms, rhos, sum_ref, near_ref, far_ref, near_in, far_in, mult_ref, side_ref, upd_ref, fac_ref,
+    terms, rhos, sum_ref, near_ref, far_ref, near_in, far_in, mult_ref, mask_ref, pieces_ref, upd_ref, fac_ref,
     mult_out, res_out, amp_out, amp_ref,
 ):
     cases, width = mult_out.shape
@@ -267,15 +301,19 @@
     amp = solve(total, lower, inverse, cases, amp_ref)
     near = near_ref[...] + near_in[...]
     far = far_ref[...] + jnp.where((me == devices - 1), 0.0, far_in[...])
-    live = side_ref[ROWS : ROWS + 1, width:]
-    contact = side_ref[ROWS + 1 : ROWS + 2, width:] > 0.0
+    live = mask_ref[0:1, width:]
+    contact = mask_ref[1:2, width:] > 0.0
     open_part = jnp.where(live > 0.0, jnp.where(even, near, far), 0.0)
-    residual = open_part - project(amp, side_ref[:ROWS, width:])
+    residual = open_part - project(amp, pieces_ref[:, width:], cases)
     update = chebyshev(residual, upd_ref[:, width:], rhos)
     mult = mult_ref[:, width:] + update
     mult_out[...] = jnp.where(contact, jnp.maximum(mult, 0.0), mult)
     res_out[...] = residual
-    amp_out[...] = jnp.transpose(amp_ref[...])[:cases, :terms]
+    amp_out[...] = amp_ref[:terms, :cases]
+
+
+def rows_of(count):
+    return math.ceil(count / ROWS) * ROWS
 
 
 def shaped(*shapes):
@@ -291,6 +329,7 @@
     order = schur.shape[1]
     terms = coarse_modes.shape[1]
     devices = lax.axis_size("group") * lax.axis_size("dev")
+    blocks = (order // LANES, order, LANES)
     slot = terms // (LANES // cases) + 1
     ring = [(i, (i + 1) % devices) for i in range(devices)]
     near_pairs = [(i, i ^ 1) for i in range(devices)]
@@ -305,17 +344,17 @@
 
     msg = pl.pallas_call(
         pack_kernel,
-        out_shape=jax.ShapeDtypeStruct((cases + 2 * ROWS, width), F32),
+        out_shape=jax.ShapeDtypeStruct((rows_of(cases + terms + 2), width), F32),
         in_specs=[SMEM, SMEM, VMEM, VMEM],
         out_specs=VMEM,
         compiler_params=params(4),
         name="pack",
-    )(active_blocks, contact_from, warm_start[0], coarse_modes[0])
+    )(active_blocks, contact_from, warm_start[0], jnp.transpose(coarse_modes, (1, 0, 2)))
     halo = lax.ppermute(msg, AXES, ring)
     high, low, own, gram_row = pl.pallas_call(
         functools.partial(first_kernel, terms),
         out_shape=shaped(
-            ((order, order), BF16), ((order, order), BF16), ((cases, order), F32), ((1, LANES), F32)
+            (blocks, BF16), (blocks, BF16), ((cases, order), F32), ((1, LANES), F32)
         ),
         in_specs=[ANY, VMEM],
         out_specs=[VMEM] * 4,
@@ -335,12 +374,12 @@
     half = ((cases, width), F32)
     full = ((cases, order), F32)
     payload = ((devices, slot, LANES), F32)
-    rows = ((math.ceil(terms * (terms + 1) // 2 / ROWS) * ROWS, LANES), F32)
-    near, far, pay_out, mult, side = pl.pallas_call(
+    rows = ((rows_of(terms * (terms + 1) // 2), LANES), F32)
+    near, far, pay_out, mult, masks, pieces = pl.pallas_call(
         functools.partial(second_kernel, terms),
-        out_shape=shaped(half, half, payload, full, ((2 * ROWS, order), F32)),
+        out_shape=shaped(half, half, payload, full, ((2, order), F32), ((3 * ROWS, order), BF16)),
         in_specs=[VMEM] * 7,
-        out_specs=[VMEM] * 5,
+        out_specs=[VMEM] * 6,
         compiler_params=params(8),
         name="second",
     )(high, low, own, halo, msg, load[0], gram_row)
@@ -353,7 +392,7 @@
         gathered = lax.all_to_all(pay_out, AXES, 0, 0)
         first = step == 0
         if step < ITERS - 1:
-            inputs = [gathered, near, far, near_in, far_in, mult, side, load[0], high, low]
+            inputs = [gathered, near, far, near_in, far_in, mult, masks, pieces, load[0], high, low]
             outputs = [half, half, payload, full, full]
             if first:
                 outputs.append(rows)
@@ -371,17 +410,17 @@
             if first:
                 factor = out[5]
         else:
-            inputs = [gathered, near, far, near_in, far_in, mult, side, update, factor]
+            inputs = [gathered, near, far, near_in, far_in, mult, masks, pieces, update, factor]
             mult, residual, amplitudes = pl.pallas_call(
                 functools.partial(last_kernel, terms, rhos[step]),
-                out_shape=shaped(half, half, ((cases, terms), F32)),
+                out_shape=shaped(half, half, ((terms, cases), F32)),
                 in_specs=[VMEM] * len(inputs),
                 out_specs=[VMEM] * 3,
                 scratch_shapes=amp_scratch,
                 compiler_params=params(8),
                 name="last",
             )(*inputs)
-    return mult[None], residual[None], amplitudes
+    return mult[None], residual[None], amplitudes.T
 
 
 def solution(mesh):

time: 61.8 us -> 59.5 us (0.963)
  Pallas kernels: 7.79 us -> 6.35 us
  local copies, waits for them, and re-layouts: 4.47 us -> 3.79 us
    pallas_call x2, Pallas kernels: 3.67 us -> 2.87 us  [shards(): pl.pallas_call(functools.partial(middle_kernel, terms, first, rhos[step])...]
    unnamed x8, local copies, waits for them, and re-layouts: 4.47 us -> 3.79 us
where the time goes in v1:
time: 59.5 us; the launch traced here: 59.2 us
  blocking collectives  35 us (59%)
  starting transfers between devices  8.93 us (15%)
  Pallas kernels  6.35 us (11%)
  local copies, waits for them, and re-layouts  3.79 us (6%)
  waiting for transfers between devices  3.12 us (5%)
  between operations  2.01 us (3%)
    all_to_all x3, blocking collectives, shards(): gathered = lax.all_to_all(pay_out, AXES, 0, 0)  35 us
    ppermute x3, starting transfers between devices, shards(): far_in = lax.ppermute(far, AXES, far_pairs)  4.14 us
    unnamed x8, local copies, waits for them, and re-layouts  3.79 us
    ppermute x1, waiting for transfers between devices, shards(): halo = lax.ppermute(msg, AXES, ring)  3.1 us
    ppermute x1, starting transfers between devices, shards(): halo = lax.ppermute(msg, AXES, ring)  3.02 us
    pallas_call x2, Pallas kernels, shards(): pl.pallas_call(functools.partial(middle_kernel, terms, first, rhos[step])...  2.87 us
    ppermute x3, starting transfers between devices, shards(): near_in = lax.ppermute(near, AXES, near_pairs)  1.77 us
    pallas_call x1, Pallas kernels, shards(): pl.pallas_call(functools.partial(first_kernel, terms), out_shape=shaped((...  1.68 us
  transfers between devices with their start and end apart: 7, of which 1 were waited for; matrix products, arithmetic and copies ran while one was open for 0% of the time, Pallas kernels for 3%

profile of v1, /device:TPU:0, one launch (start us, length us, event | category | flops | bytes accessed | tf_op | source)
XLA Modules:
  0.0 59.2 jit_solution(2191179270909560720)
XLA Ops:
  1.9 0.0 copy-start.2
  1.9 0.9 %copy-done.2 = f32[1,64,512]{2,1,0:T(8,128)S(1)} copy-done((f32[1,64,512]{2,1,0:T(8,128)S(1)}, f32[1,64,512]{2,1,0:T(8,128)}, u32[]{:S(2)}) %copy-start.2) | copy-done | bytes 131096
  2.8 0.0 copy-start.3
  2.8 0.7 %copy-done.3 = f32[1,6,512]{2,0,1:T(1,128)S(1)} copy-done((f32[1,6,512]{2,0,1:T(1,128)S(1)}, f32[1,6,512]{2,0,1:T(1,128)}, u32[]{:S(2)}) %copy-start.3) | copy-done | bytes 12312
  3.6 3.0 %collective-permute-start = (f32[72,512]{1,0:T(8,128)S(1)}, f32[72,512]{1,0:T(8,128)S(1)}, u32[]{:S(2)}, u32[]{:S(2)}) collective-permute-start(f32[72,512]{1,0:T(8,128)S(1)} %pack.1.msg_ref), channel_id=1, source_target_pairs={{0,1},{1,2},{2,3},{3,4},{4,5},{5,6},{6,7},{7,8},{8,9},{9,10},{10,1... | collective-permute-start | bytes 442376 | tf_op jit(solution)/shard_map/ppermute | solution.py:353
  6.6 0.0 copy-start
  6.6 2.2 %copy-done = f32[1,1024,1024]{2,1,0:T(8,128)S(1)} copy-done((f32[1,1024,1024]{2,1,0:T(8,128)S(1)}, f32[1,1024,1024]{2,1,0:T(8,128)}, u32[]{:S(2)}) %copy-start) | copy-done | bytes 4194328
  8.8 0.0 copy-start.1
  8.8 1.7 %first.1 = (bf16[8,1024,128]{2,1,0:T(8,128)(2,1)S(1)}, bf16[8,1024,128]{2,1,0:T(8,128)(2,1)S(1)}, f32[64,1024]{1,0:T(8,128)S(1)}, f32[1,128]{1,0:T(1,128)S(1)}) custom-call(f32[1024,1024]{1,0:T(8,128)S(1)} %bitcast.7, f32[72,512]{1,0:T(8,128)S(1)} %pack.1.msg_ref), custom_call_target="tpu_custom_call" | custom-call | flops 268435456 | bytes 8388608 | tf_op jit(solution)/shard_map/first/pallas_call | solution.py:354
  10.5 3.1 %collective-permute-done.halo_ref = f32[72,512]{1,0:T(8,128)S(1)} collective-permute-done((f32[72,512]{1,0:T(8,128)S(1)}, f32[72,512]{1,0:T(8,128)S(1)}, u32[]{:S(2)}, u32[]{:S(2)}) %collective-permute-start) | collective-permute-done | bytes 147488 | tf_op jit(solution)/shard_map/ppermute | solution.py:353
  13.6 0.0 copy-done.1
  13.6 0.7 %second.1 = (f32[64,512]{1,0:T(8,128)S(1)}, f32[64,512]{1,0:T(8,128)S(1)}, f32[32,4,128]{2,1,0:T(4,128)S(1)}, f32[64,1024]{1,0:T(8,128)S(1)}, f32[2,1024]{1,0:T(2,128)S(1)}, /*index=5*/bf16[24,1024]{1,0:T(8,128)(2,1)S(1)}) custom-call(bf16[8,1024,128]{2,1,0:T(8,128)(2,1)S(1)} %get-tuple-element.27.high_ref, ...), custom_call_target="tpu_custom_call" | custom-call | tf_op jit(solution)/shard_map/second/pallas_call | solution.py:378
  14.3 0.1 collective-permute-start.1
  14.4 2.3 %collective-permute-start.2 = (f32[64,512]{1,0:T(8,128)S(1)}, f32[64,512]{1,0:T(8,128)S(1)}, u32[]{:S(2)}, u32[]{:S(2)}) collective-permute-start(f32[64,512]{1,0:T(8,128)S(1)} %get-tuple-element.33.far_ref), channel_id=1, source_target_pairs={{0,31},{1,2},{2,1},{3,4},{4,3},{5,6},{6,5},{7,8},{8,7},{9,10},{10,... | collective-permute-start | bytes 393224 | tf_op jit(solution)/shard_map/ppermute | solution.py:390
  16.7 11.3 %all_to_all.15.sum_ref = f32[32,4,128]{2,1,0:T(4,128)S(1)} all-to-all(f32[32,4,128]{2,1,0:T(4,128)S(1)} %get-tuple-element.31), channel_id=1, replica_groups=mesh['group'=4,'dev'=8] {'group','dev'}, dimensions={0} | all-to-all | bytes 131072 | tf_op jit(solution)/shard_map/all_to_all | solution.py:392
  28.0 0.0 collective-permute-done.1.near_in
  28.0 0.0 collective-permute-done.2.far_in
  28.0 1.5 %shard_map.85 = (f32[64,512]{1,0:T(8,128)S(1)}, f32[64,512]{1,0:T(8,128)S(1)}, f32[32,4,128]{2,1,0:T(4,128)S(1)}, f32[64,1024]{1,0:T(8,128)S(1)}, f32[64,1024]{1,0:T(8,128)S(1)}, /*index=5*/f32[24,128]{1,0:T(8,128)S(1)}) custom-call(f32[32,4,128]{2,1,0:T(4,128)S(1)} %all_to_all.15.sum_ref, f32[64,512]{1,0:T(8,128)S(1)} %get-tuple-element.32.near_ref, ...), custom_call_target="tpu_custom_call" | custom-call | tf_op jit(solution)/shard_map/pallas_call | solution.py:401
  29.5 0.8 %collective-permute-start.3 = (f32[64,512]{1,0:T(8,128)S(1)}, f32[64,512]{1,0:T(8,128)S(1)}, u32[]{:S(2)}, u32[]{:S(2)}) collective-permute-start(f32[64,512]{1,0:T(8,128)S(1)} %get-tuple-element.38.near_ref), channel_id=1, source_target_pairs={{0,1},{1,0},{2,3},{3,2},{4,5},{5,4},{6,7},{7,6},{8,9},{9,8},{10,11... | collective-permute-start | bytes 393224 | tf_op jit(solution)/shard_map/ppermute | solution.py:391
  30.3 0.9 %collective-permute-start.4 = (f32[64,512]{1,0:T(8,128)S(1)}, f32[64,512]{1,0:T(8,128)S(1)}, u32[]{:S(2)}, u32[]{:S(2)}) collective-permute-start(f32[64,512]{1,0:T(8,128)S(1)} %get-tuple-element.39.far_ref), channel_id=1, source_target_pairs={{0,31},{1,2},{2,1},{3,4},{4,3},{5,6},{6,5},{7,8},{8,7},{9,10},{10,... | collective-permute-start | bytes 393224 | tf_op jit(solution)/shard_map/ppermute | solution.py:390
  31.2 11.9 %all_to_all.16.sum_ref = f32[32,4,128]{2,1,0:T(4,128)S(1)} all-to-all(f32[32,4,128]{2,1,0:T(4,128)S(1)} %get-tuple-element.37), channel_id=1, replica_groups=mesh['group'=4,'dev'=8] {'group','dev'}, dimensions={0} | all-to-all | bytes 131072 | tf_op jit(solution)/shard_map/all_to_all | solution.py:392
  43.1 0.0 collective-permute-done.3.near_in
  43.1 0.0 collective-permute-done.4.far_in
  43.1 1.4 %shard_map.86 = (f32[64,512]{1,0:T(8,128)S(1)}, f32[64,512]{1,0:T(8,128)S(1)}, f32[32,4,128]{2,1,0:T(4,128)S(1)}, f32[64,1024]{1,0:T(8,128)S(1)}, f32[64,1024]{1,0:T(8,128)S(1)}) custom-call(f32[32,4,128]{2,1,0:T(4,128)S(1)} %all_to_all.16.sum_ref, f32[64,512]{1,0:T(8,128)S(1)} %get-tuple-element.38.near_ref, f32[64,512]{1,0:T(8,128)S(1)} %get-tuple-element.39.far_ref, ...), custom_call_target="tpu_custom_call" | custom-call | tf_op jit(solution)/shard_map/pallas_call | solution.py:401
  44.5 0.8 %collective-permute-start.5 = (f32[64,512]{1,0:T(8,128)S(1)}, f32[64,512]{1,0:T(8,128)S(1)}, u32[]{:S(2)}, u32[]{:S(2)}) collective-permute-start(f32[64,512]{1,0:T(8,128)S(1)} %get-tuple-element.44.near_ref), channel_id=1, source_target_pairs={{0,1},{1,0},{2,3},{3,2},{4,5},{5,4},{6,7},{7,6},{8,9},{9,8},{10,11... | collective-permute-start | bytes 393224 | tf_op jit(solution)/shard_map/ppermute | solution.py:391
  45.4 0.9 %collective-permute-start.6 = (f32[64,512]{1,0:T(8,128)S(1)}, f32[64,512]{1,0:T(8,128)S(1)}, u32[]{:S(2)}, u32[]{:S(2)}) collective-permute-start(f32[64,512]{1,0:T(8,128)S(1)} %get-tuple-element.45.far_ref), channel_id=1, source_target_pairs={{0,31},{1,2},{2,1},{3,4},{4,3},{5,6},{6,5},{7,8},{8,7},{9,10},{10,... | collective-permute-start | bytes 393224 | tf_op jit(solution)/shard_map/ppermute | solution.py:390
  46.3 11.9 %all_to_all.17.sum_ref = f32[32,4,128]{2,1,0:T(4,128)S(1)} all-to-all(f32[32,4,128]{2,1,0:T(4,128)S(1)} %get-tuple-element.43), channel_id=1, replica_groups=mesh['group'=4,'dev'=8] {'group','dev'}, dimensions={0} | all-to-all | bytes 131072 | tf_op jit(solution)/shard_map/all_to_all | solution.py:392
  58.1 0.0 collective-permute-done.5.near_in
  58.1 0.0 collective-permute-done.6.far_in
  58.1 1.1 %last.1 = (f32[64,512]{1,0:T(8,128)}, f32[64,512]{1,0:T(8,128)}, f32[6,64]{1,0:T(8,128)}) custom-call(f32[32,4,128]{2,1,0:T(4,128)S(1)} %all_to_all.17.sum_ref, f32[64,512]{1,0:T(8,128)S(1)} %get-tuple-element.44.near_ref, f32[64,512]{1,0:T(8,128)S(1)} %get-tuple-element.45.far_ref, f32[64,512]{1,0:T(8,128)S(1)} %collective-permute-done.5.near_in, ...), custom_call_target="tpu_custom_call" | custom-call | tf_op jit(solution)/shard_map/last/pallas_call | solution.py:414
  (1 shorter events, 0.0 us)
Async XLA Ops:
  1.9 0.9 %copy-start.2 = (f32[1,64,512]{2,1,0:T(8,128)S(1)}, f32[1,64,512]{2,1,0:T(8,128)}, u32[]{:S(2)}) copy-start(f32[1,64,512]{2,1,0:T(8,128)} %param.9) | copy-start | bytes 393220
  2.8 0.7 %copy-start.3 = (f32[1,6,512]{2,0,1:T(1,128)S(1)}, f32[1,6,512]{2,0,1:T(1,128)}, u32[]{:S(2)}) copy-start(f32[1,6,512]{2,0,1:T(1,128)} %param.7) | copy-start | bytes 36868
  3.6 10.0 %collective-permute-start = (f32[72,512]{1,0:T(8,128)S(1)}, f32[72,512]{1,0:T(8,128)S(1)}, u32[]{:S(2)}, u32[]{:S(2)}) collective-permute-start(f32[72,512]{1,0:T(8,128)S(1)} %pack.1.msg_ref), channel_id=1, source_target_pairs={{0,1},{1,2},{2,3},{3,4},{4,5},{5,6},{6,7},{7,8},{8,9},{9,10},{10,1... | collective-permute-start | bytes 442376 | tf_op jit(solution)/shard_map/ppermute | solution.py:353
  6.6 2.2 %copy-start = (f32[1,1024,1024]{2,1,0:T(8,128)S(1)}, f32[1,1024,1024]{2,1,0:T(8,128)}, u32[]{:S(2)}) copy-start(f32[1,1024,1024]{2,1,0:T(8,128)} %param.6) | copy-start | bytes 12582916
  8.8 4.8 %copy-start.1 = (f32[1,64,512]{2,1,0:T(8,128)S(1)}, f32[1,64,512]{2,1,0:T(8,128)}, u32[]{:S(2)}) copy-start(f32[1,64,512]{2,1,0:T(8,128)} %param.8) | copy-start | bytes 393220
  14.3 13.7 %collective-permute-start.1 = (f32[64,512]{1,0:T(8,128)S(1)}, f32[64,512]{1,0:T(8,128)S(1)}, u32[]{:S(2)}, u32[]{:S(2)}) collective-permute-start(f32[64,512]{1,0:T(8,128)S(1)} %get-tuple-element.32.near_ref), channel_id=1, source_target_pairs={{0,1},{1,0},{2,3},{3,2},{4,5},{5,4},{6,7},{7,6},{8,9},{9,8},{10,11... | collective-permute-start | bytes 393224 | tf_op jit(solution)/shard_map/ppermute | solution.py:391
  14.4 13.6 %collective-permute-start.2 = (f32[64,512]{1,0:T(8,128)S(1)}, f32[64,512]{1,0:T(8,128)S(1)}, u32[]{:S(2)}, u32[]{:S(2)}) collective-permute-start(f32[64,512]{1,0:T(8,128)S(1)} %get-tuple-element.33.far_ref), channel_id=1, source_target_pairs={{0,31},{1,2},{2,1},{3,4},{4,3},{5,6},{6,5},{7,8},{8,7},{9,10},{10,... | collective-permute-start | bytes 393224 | tf_op jit(solution)/shard_map/ppermute | solution.py:390
  29.5 13.6 %collective-permute-start.3 = (f32[64,512]{1,0:T(8,128)S(1)}, f32[64,512]{1,0:T(8,128)S(1)}, u32[]{:S(2)}, u32[]{:S(2)}) collective-permute-start(f32[64,512]{1,0:T(8,128)S(1)} %get-tuple-element.38.near_ref), channel_id=1, source_target_pairs={{0,1},{1,0},{2,3},{3,2},{4,5},{5,4},{6,7},{7,6},{8,9},{9,8},{10,11... | collective-permute-start | bytes 393224 | tf_op jit(solution)/shard_map/ppermute | solution.py:391
  30.3 12.8 %collective-permute-start.4 = (f32[64,512]{1,0:T(8,128)S(1)}, f32[64,512]{1,0:T(8,128)S(1)}, u32[]{:S(2)}, u32[]{:S(2)}) collective-permute-start(f32[64,512]{1,0:T(8,128)S(1)} %get-tuple-element.39.far_ref), channel_id=1, source_target_pairs={{0,31},{1,2},{2,1},{3,4},{4,3},{5,6},{6,5},{7,8},{8,7},{9,10},{10,... | collective-permute-start | bytes 393224 | tf_op jit(solution)/shard_map/ppermute | solution.py:390
  44.5 13.6 %collective-permute-start.5 = (f32[64,512]{1,0:T(8,128)S(1)}, f32[64,512]{1,0:T(8,128)S(1)}, u32[]{:S(2)}, u32[]{:S(2)}) collective-permute-start(f32[64,512]{1,0:T(8,128)S(1)} %get-tuple-element.44.near_ref), channel_id=1, source_target_pairs={{0,1},{1,0},{2,3},{3,2},{4,5},{5,4},{6,7},{7,6},{8,9},{9,8},{10,11... | collective-permute-start | bytes 393224 | tf_op jit(solution)/shard_map/ppermute | solution.py:391
  45.4 12.8 %collective-permute-start.6 = (f32[64,512]{1,0:T(8,128)S(1)}, f32[64,512]{1,0:T(8,128)S(1)}, u32[]{:S(2)}, u32[]{:S(2)}) collective-permute-start(f32[64,512]{1,0:T(8,128)S(1)} %get-tuple-element.45.far_ref), channel_id=1, source_target_pairs={{0,31},{1,2},{2,1},{3,4},{4,3},{5,6},{6,5},{7,8},{8,7},{9,10},{10,... | collective-permute-start | bytes 393224 | tf_op jit(solution)/shard_map/ppermute | solution.py:390

commit v2 on v1

--- a/solution.py
+++ b/solution.py
@@ -25,7 +25,7 @@
 HIGHEST = lax.Precision.HIGHEST
 VMEM = pl.BlockSpec(memory_space=pltpu.VMEM)
 SMEM = pl.BlockSpec(memory_space=pltpu.SMEM)
-ANY = pl.BlockSpec(memory_space=pl.ANY)
+HBM = pl.BlockSpec(memory_space=pltpu.HBM)
 
 
 def split(x):
@@ -69,7 +69,13 @@
     return me, lax.axis_size("group") * lax.axis_size("dev")
 
 
-def pack_kernel(count_ref, from_ref, warm_ref, modes_ref, out_ref):
+def pack_kernel(count_ref, from_ref, warm_hbm, modes_hbm, out_ref, warm_ref, modes_ref, sems):
+    copies = [
+        pltpu.make_async_copy(source, target, sems.at[n])
+        for n, (source, target) in enumerate(((warm_hbm, warm_ref), (modes_hbm, modes_ref)))
+    ]
+    for copy in copies:
+        copy.start()
     cases, width = warm_ref.shape
     terms = modes_ref.shape[0]
     spare = out_ref.shape[0] - cases - terms
@@ -77,6 +83,8 @@
     alive = dofs < count_ref[0] * BLK
     live = alive.astype(F32)
     contact = (alive & (dofs >= from_ref[0])).astype(F32)
+    for copy in copies:
+        copy.wait()
     out_ref[:cases, :] = warm_ref[...] * live
     for c in range(terms):
         out_ref[cases + c : cases + c + 1, :] = modes_ref[c] * live
@@ -320,6 +328,10 @@
     return [jax.ShapeDtypeStruct(s, d) for s, d in shapes]
 
 
+def in_hbm(x):
+    return pltpu.with_memory_space_constraint(x, pltpu.HBM)
+
+
 def params(megabytes):
     return pltpu.CompilerParams(vmem_limit_bytes=megabytes << 20)
 
@@ -345,18 +357,23 @@
     msg = pl.pallas_call(
         pack_kernel,
         out_shape=jax.ShapeDtypeStruct((rows_of(cases + terms + 2), width), F32),
-        in_specs=[SMEM, SMEM, VMEM, VMEM],
+        in_specs=[SMEM, SMEM, HBM, HBM],
         out_specs=VMEM,
+        scratch_shapes=[
+            pltpu.VMEM((cases, width), F32),
+            pltpu.VMEM((terms, 1, width), F32),
+            pltpu.SemaphoreType.DMA((2,)),
+        ],
         compiler_params=params(4),
         name="pack",
-    )(active_blocks, contact_from, warm_start[0], jnp.transpose(coarse_modes, (1, 0, 2)))
+    )(active_blocks, contact_from, in_hbm(warm_start[0]), in_hbm(jnp.transpose(coarse_modes, (1, 0, 2))))
     halo = lax.ppermute(msg, AXES, ring)
     high, low, own, gram_row = pl.pallas_call(
         functools.partial(first_kernel, terms),
         out_shape=shaped(
             (blocks, BF16), (blocks, BF16), ((cases, order), F32), ((1, LANES), F32)
         ),
-        in_specs=[ANY, VMEM],
+        in_specs=[HBM, VMEM],
         out_specs=[VMEM] * 4,
         scratch_shapes=[
             pltpu.VMEM((order, order), F32),
@@ -369,7 +386,7 @@
             flops=4 * cases * order * order, bytes_accessed=8 * order * order, transcendentals=0
         ),
         name="first",
-    )(schur[0], msg)
+    )(in_hbm(schur[0]), msg)
 
     half = ((cases, width), F32)
     full = ((cases, order), F32)

time: 59.5 us -> 58.7 us (0.987)
  local copies, waits for them, and re-layouts: 3.79 us -> 0.01 us
  Pallas kernels: 6.35 us -> 7.94 us
  waiting for transfers between devices: 3.12 us -> 4.64 us
    unnamed x8 -> x2, local copies, waits for them, and re-layouts: 3.79 us -> 0.01 us
    ppermute x1, waiting for transfers between devices: 3.1 us -> 4.62 us  [shards(): halo = lax.ppermute(msg, AXES, ring)]
    pallas_call x1, Pallas kernels: 0.02 us -> 0.94 us  [shards(): pl.pallas_call(pack_kernel, out_shape=jax.ShapeDtypeStruct((rows_of(cases...]
    pallas_call x1, Pallas kernels: 1.68 us -> 2.35 us  [shards(): pl.pallas_call(functools.partial(first_kernel, terms), out_shape=shaped((...]
  transfers between devices with their start and end apart: 7 -> 7, of which waited for: 1 -> 1; matrix products, arithmetic and copies ran while one was open for 0% -> 0% of each run, Pallas kernels for 3% -> 4%
where the time goes in v2:
time: 58.7 us; the launch traced here: 58.5 us
  blocking collectives  35 us (60%)
  starting transfers between devices  8.91 us (15%)
  Pallas kernels  7.94 us (14%)
  waiting for transfers between devices  4.64 us (8%)
  between operations  2.01 us (3%)
    all_to_all x3, blocking collectives, shards(): gathered = lax.all_to_all(pay_out, AXES, 0, 0)  35 us
    ppermute x1, waiting for transfers between devices, shards(): halo = lax.ppermute(msg, AXES, ring)  4.62 us
    ppermute x3, starting transfers between devices, shards(): far_in = lax.ppermute(far, AXES, far_pairs)  4.14 us
    ppermute x1, starting transfers between devices, shards(): halo = lax.ppermute(msg, AXES, ring)  3.02 us
    pallas_call x2, Pallas kernels, shards(): pl.pallas_call(functools.partial(middle_kernel, terms, first, rhos[step])...  2.87 us
    pallas_call x1, Pallas kernels, shards(): pl.pallas_call(functools.partial(first_kernel, terms), out_shape=shaped((...  2.35 us
    ppermute x3, starting transfers between devices, shards(): near_in = lax.ppermute(near, AXES, near_pairs)  1.75 us
  transfers between devices with their start and end apart: 7, of which 1 were waited for; matrix products, arithmetic and copies ran while one was open for 0% of the time, Pallas kernels for 4%

profile of v2, /device:TPU:0, one launch (start us, length us, event | category | flops | bytes accessed | tf_op | source)
XLA Modules:
  0.0 58.5 jit_solution(4073382087631061934)
XLA Ops:
  1.9 0.9 %pack.1.msg_ref = f32[72,512]{1,0:T(8,128)S(1)} custom-call(s32[1]{0:T(128)S(6)} %copy.9.count_ref, s32[1]{0:T(128)S(6)} %copy.10.from_ref, f32[64,512]{1,0:T(8,128)} %bitcast.11, f32[6,1,512]{2,1,0:T(1,128)} %bitcast.12), custom_call_target="tpu_custom_call" | custom-call | tf_op jit(solution)/shard_map/pack/pallas_call | solution.py:357
  2.9 3.0 %collective-permute-start = (f32[72,512]{1,0:T(8,128)S(1)}, f32[72,512]{1,0:T(8,128)S(1)}, u32[]{:S(2)}, u32[]{:S(2)}) collective-permute-start(f32[72,512]{1,0:T(8,128)S(1)} %pack.1.msg_ref), channel_id=1, source_target_pairs={{0,1},{1,2},{2,3},{3,4},{4,5},{5,6},{6,7},{7,8},{8,9},{9,10},{10,1... | collective-permute-start | bytes 442376 | tf_op jit(solution)/shard_map/ppermute | solution.py:370
  5.9 0.0 copy-start
  5.9 2.4 %first.1 = (bf16[8,1024,128]{2,1,0:T(8,128)(2,1)S(1)}, bf16[8,1024,128]{2,1,0:T(8,128)(2,1)S(1)}, f32[64,1024]{1,0:T(8,128)S(1)}, f32[1,128]{1,0:T(1,128)S(1)}) custom-call(f32[1024,1024]{1,0:T(8,128)} %bitcast.10, f32[72,512]{1,0:T(8,128)S(1)} %pack.1.msg_ref), custom_call_target="tpu_custom_call" | custom-call | flops 268435456 | bytes 8388608 | tf_op jit(solution)/shard_map/first/pallas_call | solution.py:371
  8.3 4.6 %collective-permute-done.halo_ref = f32[72,512]{1,0:T(8,128)S(1)} collective-permute-done((f32[72,512]{1,0:T(8,128)S(1)}, f32[72,512]{1,0:T(8,128)S(1)}, u32[]{:S(2)}, u32[]{:S(2)}) %collective-permute-start) | collective-permute-done | bytes 147488 | tf_op jit(solution)/shard_map/ppermute | solution.py:370
  12.9 0.0 copy-done
  12.9 0.7 %second.1 = (f32[64,512]{1,0:T(8,128)S(1)}, f32[64,512]{1,0:T(8,128)S(1)}, f32[32,4,128]{2,1,0:T(4,128)S(1)}, f32[64,1024]{1,0:T(8,128)S(1)}, f32[2,1024]{1,0:T(2,128)S(1)}, /*index=5*/bf16[24,1024]{1,0:T(8,128)(2,1)S(1)}) custom-call(bf16[8,1024,128]{2,1,0:T(8,128)(2,1)S(1)} %get-tuple-element.27.high_ref, ...), custom_call_target="tpu_custom_call" | custom-call | tf_op jit(solution)/shard_map/second/pallas_call | solution.py:395
  13.6 0.1 collective-permute-start.1
  13.7 2.3 %collective-permute-start.2 = (f32[64,512]{1,0:T(8,128)S(1)}, f32[64,512]{1,0:T(8,128)S(1)}, u32[]{:S(2)}, u32[]{:S(2)}) collective-permute-start(f32[64,512]{1,0:T(8,128)S(1)} %get-tuple-element.33.far_ref), channel_id=1, source_target_pairs={{0,31},{1,2},{2,1},{3,4},{4,3},{5,6},{6,5},{7,8},{8,7},{9,10},{10,... | collective-permute-start | bytes 393224 | tf_op jit(solution)/shard_map/ppermute | solution.py:407
  16.0 11.3 %all_to_all.15.sum_ref = f32[32,4,128]{2,1,0:T(4,128)S(1)} all-to-all(f32[32,4,128]{2,1,0:T(4,128)S(1)} %get-tuple-element.31), channel_id=1, replica_groups=mesh['group'=4,'dev'=8] {'group','dev'}, dimensions={0} | all-to-all | bytes 131072 | tf_op jit(solution)/shard_map/all_to_all | solution.py:409
  27.3 0.0 collective-permute-done.1.near_in
  27.3 0.0 collective-permute-done.2.far_in
  27.3 1.5 %shard_map.85 = (f32[64,512]{1,0:T(8,128)S(1)}, f32[64,512]{1,0:T(8,128)S(1)}, f32[32,4,128]{2,1,0:T(4,128)S(1)}, f32[64,1024]{1,0:T(8,128)S(1)}, f32[64,1024]{1,0:T(8,128)S(1)}, /*index=5*/f32[24,128]{1,0:T(8,128)S(1)}) custom-call(f32[32,4,128]{2,1,0:T(4,128)S(1)} %all_to_all.15.sum_ref, f32[64,512]{1,0:T(8,128)S(1)} %get-tuple-element.32.near_ref, ...), custom_call_target="tpu_custom_call" | custom-call | tf_op jit(solution)/shard_map/pallas_call | solution.py:418
  28.8 0.8 %collective-permute-start.3 = (f32[64,512]{1,0:T(8,128)S(1)}, f32[64,512]{1,0:T(8,128)S(1)}, u32[]{:S(2)}, u32[]{:S(2)}) collective-permute-start(f32[64,512]{1,0:T(8,128)S(1)} %get-tuple-element.38.near_ref), channel_id=1, source_target_pairs={{0,1},{1,0},{2,3},{3,2},{4,5},{5,4},{6,7},{7,6},{8,9},{9,8},{10,11... | collective-permute-start | bytes 393224 | tf_op jit(solution)/shard_map/ppermute | solution.py:408
  29.6 0.9 %collective-permute-start.4 = (f32[64,512]{1,0:T(8,128)S(1)}, f32[64,512]{1,0:T(8,128)S(1)}, u32[]{:S(2)}, u32[]{:S(2)}) collective-permute-start(f32[64,512]{1,0:T(8,128)S(1)} %get-tuple-element.39.far_ref), channel_id=1, source_target_pairs={{0,31},{1,2},{2,1},{3,4},{4,3},{5,6},{6,5},{7,8},{8,7},{9,10},{10,... | collective-permute-start | bytes 393224 | tf_op jit(solution)/shard_map/ppermute | solution.py:407
  30.5 11.9 %all_to_all.16.sum_ref = f32[32,4,128]{2,1,0:T(4,128)S(1)} all-to-all(f32[32,4,128]{2,1,0:T(4,128)S(1)} %get-tuple-element.37), channel_id=1, replica_groups=mesh['group'=4,'dev'=8] {'group','dev'}, dimensions={0} | all-to-all | bytes 131072 | tf_op jit(solution)/shard_map/all_to_all | solution.py:409
  42.4 0.0 collective-permute-done.3.near_in
  42.4 0.0 collective-permute-done.4.far_in
  42.4 1.4 %shard_map.86 = (f32[64,512]{1,0:T(8,128)S(1)}, f32[64,512]{1,0:T(8,128)S(1)}, f32[32,4,128]{2,1,0:T(4,128)S(1)}, f32[64,1024]{1,0:T(8,128)S(1)}, f32[64,1024]{1,0:T(8,128)S(1)}) custom-call(f32[32,4,128]{2,1,0:T(4,128)S(1)} %all_to_all.16.sum_ref, f32[64,512]{1,0:T(8,128)S(1)} %get-tuple-element.38.near_ref, f32[64,512]{1,0:T(8,128)S(1)} %get-tuple-element.39.far_ref, ...), custom_call_target="tpu_custom_call" | custom-call | tf_op jit(solution)/shard_map/pallas_call | solution.py:418
  43.8 0.9 %collective-permute-start.5 = (f32[64,512]{1,0:T(8,128)S(1)}, f32[64,512]{1,0:T(8,128)S(1)}, u32[]{:S(2)}, u32[]{:S(2)}) collective-permute-start(f32[64,512]{1,0:T(8,128)S(1)} %get-tuple-element.44.near_ref), channel_id=1, source_target_pairs={{0,1},{1,0},{2,3},{3,2},{4,5},{5,4},{6,7},{7,6},{8,9},{9,8},{10,11... | collective-permute-start | bytes 393224 | tf_op jit(solution)/shard_map/ppermute | solution.py:408
  44.7 0.9 %collective-permute-start.6 = (f32[64,512]{1,0:T(8,128)S(1)}, f32[64,512]{1,0:T(8,128)S(1)}, u32[]{:S(2)}, u32[]{:S(2)}) collective-permute-start(f32[64,512]{1,0:T(8,128)S(1)} %get-tuple-element.45.far_ref), channel_id=1, source_target_pairs={{0,31},{1,2},{2,1},{3,4},{4,3},{5,6},{6,5},{7,8},{8,7},{9,10},{10,... | collective-permute-start | bytes 393224 | tf_op jit(solution)/shard_map/ppermute | solution.py:407
  45.6 11.9 %all_to_all.17.sum_ref = f32[32,4,128]{2,1,0:T(4,128)S(1)} all-to-all(f32[32,4,128]{2,1,0:T(4,128)S(1)} %get-tuple-element.43), channel_id=1, replica_groups=mesh['group'=4,'dev'=8] {'group','dev'}, dimensions={0} | all-to-all | bytes 131072 | tf_op jit(solution)/shard_map/all_to_all | solution.py:409
  57.4 0.0 collective-permute-done.5.near_in
  57.4 0.0 collective-permute-done.6.far_in
  57.4 1.1 %last.1 = (f32[64,512]{1,0:T(8,128)}, f32[64,512]{1,0:T(8,128)}, f32[6,64]{1,0:T(8,128)}) custom-call(f32[32,4,128]{2,1,0:T(4,128)S(1)} %all_to_all.17.sum_ref, f32[64,512]{1,0:T(8,128)S(1)} %get-tuple-element.44.near_ref, f32[64,512]{1,0:T(8,128)S(1)} %get-tuple-element.45.far_ref, f32[64,512]{1,0:T(8,128)S(1)} %collective-permute-done.5.near_in, ...), custom_call_target="tpu_custom_call" | custom-call | tf_op jit(solution)/shard_map/last/pallas_call | solution.py:431
Async XLA Ops:
  2.9 10.0 %collective-permute-start = (f32[72,512]{1,0:T(8,128)S(1)}, f32[72,512]{1,0:T(8,128)S(1)}, u32[]{:S(2)}, u32[]{:S(2)}) collective-permute-start(f32[72,512]{1,0:T(8,128)S(1)} %pack.1.msg_ref), channel_id=1, source_target_pairs={{0,1},{1,2},{2,3},{3,4},{4,5},{5,6},{6,7},{7,8},{8,9},{9,10},{10,1... | collective-permute-start | bytes 442376 | tf_op jit(solution)/shard_map/ppermute | solution.py:370
  5.9 7.0 %copy-start = (f32[1,64,512]{2,1,0:T(8,128)S(1)}, f32[1,64,512]{2,1,0:T(8,128)}, u32[]{:S(2)}) copy-start(f32[1,64,512]{2,1,0:T(8,128)} %param.8) | copy-start | bytes 393220
  13.6 13.7 %collective-permute-start.1 = (f32[64,512]{1,0:T(8,128)S(1)}, f32[64,512]{1,0:T(8,128)S(1)}, u32[]{:S(2)}, u32[]{:S(2)}) collective-permute-start(f32[64,512]{1,0:T(8,128)S(1)} %get-tuple-element.32.near_ref), channel_id=1, source_target_pairs={{0,1},{1,0},{2,3},{3,2},{4,5},{5,4},{6,7},{7,6},{8,9},{9,8},{10,11... | collective-permute-start | bytes 393224 | tf_op jit(solution)/shard_map/ppermute | solution.py:408
  13.7 13.6 %collective-permute-start.2 = (f32[64,512]{1,0:T(8,128)S(1)}, f32[64,512]{1,0:T(8,128)S(1)}, u32[]{:S(2)}, u32[]{:S(2)}) collective-permute-start(f32[64,512]{1,0:T(8,128)S(1)} %get-tuple-element.33.far_ref), channel_id=1, source_target_pairs={{0,31},{1,2},{2,1},{3,4},{4,3},{5,6},{6,5},{7,8},{8,7},{9,10},{10,... | collective-permute-start | bytes 393224 | tf_op jit(solution)/shard_map/ppermute | solution.py:407
  28.8 13.6 %collective-permute-start.3 = (f32[64,512]{1,0:T(8,128)S(1)}, f32[64,512]{1,0:T(8,128)S(1)}, u32[]{:S(2)}, u32[]{:S(2)}) collective-permute-start(f32[64,512]{1,0:T(8,128)S(1)} %get-tuple-element.38.near_ref), channel_id=1, source_target_pairs={{0,1},{1,0},{2,3},{3,2},{4,5},{5,4},{6,7},{7,6},{8,9},{9,8},{10,11... | collective-permute-start | bytes 393224 | tf_op jit(solution)/shard_map/ppermute | solution.py:408
  29.6 12.8 %collective-permute-start.4 = (f32[64,512]{1,0:T(8,128)S(1)}, f32[64,512]{1,0:T(8,128)S(1)}, u32[]{:S(2)}, u32[]{:S(2)}) collective-permute-start(f32[64,512]{1,0:T(8,128)S(1)} %get-tuple-element.39.far_ref), channel_id=1, source_target_pairs={{0,31},{1,2},{2,1},{3,4},{4,3},{5,6},{6,5},{7,8},{8,7},{9,10},{10,... | collective-permute-start | bytes 393224 | tf_op jit(solution)/shard_map/ppermute | solution.py:407
  43.8 13.6 %collective-permute-start.5 = (f32[64,512]{1,0:T(8,128)S(1)}, f32[64,512]{1,0:T(8,128)S(1)}, u32[]{:S(2)}, u32[]{:S(2)}) collective-permute-start(f32[64,512]{1,0:T(8,128)S(1)} %get-tuple-element.44.near_ref), channel_id=1, source_target_pairs={{0,1},{1,0},{2,3},{3,2},{4,5},{5,4},{6,7},{7,6},{8,9},{9,8},{10,11... | collective-permute-start | bytes 393224 | tf_op jit(solution)/shard_map/ppermute | solution.py:408
  44.7 12.8 %collective-permute-start.6 = (f32[64,512]{1,0:T(8,128)S(1)}, f32[64,512]{1,0:T(8,128)S(1)}, u32[]{:S(2)}, u32[]{:S(2)}) collective-permute-start(f32[64,512]{1,0:T(8,128)S(1)} %get-tuple-element.45.far_ref), channel_id=1, source_target_pairs={{0,31},{1,2},{2,1},{3,4},{4,3},{5,6},{6,5},{7,8},{8,7},{9,10},{10,... | collective-permute-start | bytes 393224 | tf_op jit(solution)/shard_map/ppermute | solution.py:407

commit v3 on v2

--- a/solution.py
+++ b/solution.py
@@ -20,6 +20,9 @@
 LANES = 128
 ROWS = 8
 CHUNK = 128
+DEPTH = 256
+WIDE = 256
+LAG = 2
 F32 = jnp.float32
 BF16 = jnp.bfloat16
 HIGHEST = lax.Precision.HIGHEST
@@ -51,17 +54,15 @@
     return both[:cases] + (both[cases:] + dot(x_high, low))
 
 
-def wide_product(x, high_ref, low_ref, start):
-    cases, depth = x.shape
-    x_high, x_low = split(x)
-    both = jnp.concatenate([x_high, x_low], axis=0)
-    out = []
-    for j in range(0, high_ref.shape[0], 2):
-        high = jnp.concatenate([high_ref[j + p, start : start + depth, :] for p in range(2)], axis=1)
-        low = jnp.concatenate([low_ref[j + p, start : start + depth, :] for p in range(2)], axis=1)
-        first = dot(both, high)
-        out.append(first[:cases] + (first[cases:] + dot(x_high, low)))
-    return jnp.concatenate(out, axis=1)
+def block_product(both, high_ref, low_ref, start, n):
+    cases, depth = both.shape[0] // 2, both.shape[1]
+    at = n * (WIDE // LANES)
+    high, low = (
+        jnp.concatenate([ref[at + p, start : start + depth, :] for p in range(WIDE // LANES)], axis=1)
+        for ref in (high_ref, low_ref)
+    )
+    first = dot(both, high)
+    return first[:cases] + (first[cases:] + dot(both[:cases], low))
 
 
 def position():
@@ -134,24 +135,33 @@
     own_ref[...] = acc[...]
 
 
-def send(even, left_half, right_half, near_ref, far_ref):
-    near_ref[...] = jnp.where(even, right_half, left_half)
-    far_ref[...] = jnp.where(even, left_half, right_half)
-
-
-def pay(terms, pieces, z2, gram_row, pay_ref):
-    cases = z2.shape[0]
+def finish(block, terms, even, load_ref, pieces, gram_row, near_ref, far_ref, pay_ref):
+    cases, width = load_ref.shape
+    count = 2 * width // WIDE
+    across = (((1,), (1,)), ((), ()))
+    z = []
+    top = low = 0.0
+    for n in range(count + LAG):
+        if n < count:
+            value = block(n)
+            if n * WIDE >= width:
+                cols = slice(n * WIDE - width, (n + 1) * WIDE - width)
+                partner = z[n - count // 2]
+                value = load_ref[:, cols] - value
+                near_ref[:, cols] = jnp.where(even, value, partner)
+                far_ref[:, cols] = jnp.where(even, partner, value)
+            z.append(value)
+        if n >= LAG:
+            part = pieces[:, (n - LAG) * WIDE : (n - LAG + 1) * WIDE]
+            z_high, z_low = split(z[n - LAG])
+            top = top + lax.dot_general(part, z_high, across, preferred_element_type=F32)
+            low = low + lax.dot_general(part, z_low, across, preferred_element_type=F32)
+    coef = top[:ROWS] + ((top[ROWS : 2 * ROWS] + low[:ROWS]) + (top[2 * ROWS : 3 * ROWS] + low[ROWS : 2 * ROWS]))
     per_row = LANES // cases
-    across = (((1,), (1,)), ((), ()))
-    z_high, z_low = split(z2)
-    top = lax.dot_general(pieces, z_high, across, preferred_element_type=F32)
-    low = lax.dot_general(pieces, z_low, across, preferred_element_type=F32)
-    coef = top[:ROWS] + ((top[ROWS : 2 * ROWS] + low[:ROWS]) + (top[2 * ROWS : 3 * ROWS] + low[ROWS : 2 * ROWS]))
     used = terms // per_row
-    parts = [coef[p * used : (p + 1) * used, :] for p in range(per_row)]
-    block = jnp.concatenate(parts, axis=1)
+    lines = jnp.concatenate([coef[p * used : (p + 1) * used, :] for p in range(per_row)], axis=1)
     slots = pay_ref.shape[0]
-    pay_ref[:, :used, :] = jnp.broadcast_to(block[None], (slots, used, LANES))
+    pay_ref[:, :used, :] = jnp.broadcast_to(lines[None], (slots, used, LANES))
     pay_ref[:, used : used + 1, :] = jnp.broadcast_to(gram_row[None], (slots, 1, LANES))
 
 
@@ -159,21 +169,22 @@
     terms, high_ref, low_ref, own_ref, halo_ref, msg_ref, load_ref, gram_ref,
     near_ref, far_ref, pay_ref, mult_ref, mask_ref, pieces_ref,
 ):
-    cases, width = load_ref.shape
+    cases, _ = load_ref.shape
     me, _ = position()
     halo = jnp.where(me > 0, halo_ref[...], 0.0)
     left = halo[:cases]
-    y = own_ref[...] - wide_product(left, high_ref, low_ref, 0)
-    y_left = y[:, :width]
-    rest = load_ref[...] - y[:, width:]
     tail = halo_ref.shape[0] - 2
     mask_ref[0:2, :] = jnp.concatenate([halo[tail:], msg_ref[tail:, :]], axis=1)
     modes = jnp.concatenate([halo[cases : cases + ROWS], msg_ref[cases : cases + ROWS, :]], axis=1)
     modes = jnp.where(lax.broadcasted_iota(jnp.int32, modes.shape, 0) < terms, modes, 0.0)
     pieces = jnp.concatenate(split3(modes), axis=0)
     pieces_ref[...] = pieces
-    send(me % 2 == 0, y_left, rest, near_ref, far_ref)
-    pay(terms, pieces, jnp.concatenate([y_left, rest], axis=1), gram_ref[...], pay_ref)
+    both = jnp.concatenate(split(left), axis=0)
+
+    def block(n):
+        return own_ref[:, n * WIDE : (n + 1) * WIDE] - block_product(both, high_ref, low_ref, 0, n)
+
+    finish(block, terms, me % 2 == 0, load_ref, pieces, gram_ref[...], near_ref, far_ref, pay_ref)
     mult_ref[...] = jnp.concatenate([left, msg_ref[:cases, :]], axis=1)
 
 
@@ -250,12 +261,14 @@
     return rho_new * rho * update + 2.0 * rho_new / DELTA * residual
 
 
-def project(amp, pieces, cases):
+def amplitudes_of(amp, cases):
     one, two, three = (p.astype(F32) for p in split3(amp))
-    left = jnp.transpose(jnp.concatenate([one, two, three, one, two, one], axis=0))[:cases]
+    return jnp.transpose(jnp.concatenate([one, two, three, one, two, one], axis=0))[:cases].astype(BF16)
+
+
+def stacked(pieces):
     m = [pieces[p * ROWS : (p + 1) * ROWS] for p in range(3)]
-    right = jnp.concatenate([m[0], m[0], m[0], m[1], m[1], m[2]], axis=0)
-    return dot(left.astype(BF16), right)
+    return jnp.concatenate([m[0], m[0], m[0], m[1], m[1], m[2]], axis=0)
 
 
 def middle_kernel(
@@ -263,9 +276,9 @@
     high_ref, low_ref, *rest,
 ):
     if first:
-        near_out, far_out, pay_ref, mult_out, upd_out, fac_out, amp_ref = rest
+        near_out, far_out, pay_ref, mult_out, upd_out, fac_out, amp_ref, coarse_ref = rest
     else:
-        upd_ref, fac_ref, near_out, far_out, pay_ref, mult_out, upd_out, amp_ref = rest
+        upd_ref, fac_ref, near_out, far_out, pay_ref, mult_out, upd_out, amp_ref, coarse_ref = rest
     cases, width = load_ref.shape
     me, devices = position()
     even = me % 2 == 0
@@ -276,48 +289,63 @@
         store_factor(lower, inverse, fac_out)
     else:
         lower, inverse = load_factor(terms, fac_ref)
-    amp = solve(total, lower, inverse, cases, amp_ref)
-    near = near_ref[...] + near_in[...]
-    far = far_ref[...] + jnp.where((me == devices - 1), 0.0, far_in[...])
-    live = mask_ref[0:1, :]
-    contact = mask_ref[1:2, :] > 0.0
+    amp = amplitudes_of(solve(total, lower, inverse, cases, amp_ref), cases)
     pieces = pieces_ref[...]
-    open_part = jnp.concatenate([jnp.where(even, far, near), jnp.where(even, near, far)], axis=1)
-    open_part = jnp.where(live > 0.0, open_part, 0.0)
-    residual = open_part - project(amp, pieces, cases)
-    update = chebyshev(residual, None if first else upd_ref[...], rhos)
-    mult = mult_ref[...] + update
-    mult = jnp.where(contact, jnp.maximum(mult, 0.0), mult)
-    mult_out[...] = mult
-    upd_out[...] = update
-    y = wide_product(jnp.concatenate([-mult[:, :width], mult[:, width:]], axis=1), high_ref, low_ref, 0)
-    y_left = y[:, :width]
-    rest_part = load_ref[...] - y[:, width:]
-    send(even, y_left, rest_part, near_out, far_out)
-    pay(terms, pieces, jnp.concatenate([y_left, rest_part], axis=1), jnp.zeros((1, LANES), F32), pay_ref)
+    coarse_ref[...] = dot(amp, stacked(pieces))
+    is_last = me == devices - 1
+    y = []
+    for start in range(0, 2 * width, DEPTH):
+        lanes = slice(start, start + DEPTH)
+        half = slice(start % width, start % width + DEPTH)
+        near = near_ref[:, half] + near_in[:, half]
+        far = far_ref[:, half] + jnp.where(is_last, 0.0, far_in[:, half])
+        open_part = jnp.where(even, far, near) if start < width else jnp.where(even, near, far)
+        open_part = jnp.where(mask_ref[0:1, lanes] > 0.0, open_part, 0.0)
+        residual = open_part - coarse_ref[:, lanes]
+        update = chebyshev(residual, None if first else upd_ref[:, lanes], rhos)
+        mult = mult_ref[:, lanes] + update
+        mult = jnp.where(mask_ref[1:2, lanes] > 0.0, jnp.maximum(mult, 0.0), mult)
+        mult_out[:, lanes] = mult
+        upd_out[:, lanes] = update
+        both = jnp.concatenate(split(-mult if start < width else mult), axis=0)
+        if start + DEPTH < 2 * width:
+            parts = [block_product(both, high_ref, low_ref, start, n) for n in range(2 * width // WIDE)]
+            y = [a + b for a, b in zip(y, parts)] if y else parts
+
+    def block(n):
+        return y[n] + block_product(both, high_ref, low_ref, start, n)
+
+    no_gram = jnp.zeros((1, LANES), F32)
+    finish(block, terms, even, load_ref, pieces, no_gram, near_out, far_out, pay_ref)
 
 
 def last_kernel(
     terms, rhos, sum_ref, near_ref, far_ref, near_in, far_in, mult_ref, mask_ref, pieces_ref, upd_ref, fac_ref,
-    mult_out, res_out, amp_out, amp_ref,
+    mult_hbm, res_hbm, amp_out, amp_ref, mult_out, res_out, sems,
 ):
     cases, width = mult_out.shape
     me, devices = position()
     even = me % 2 == 0
     total = jnp.sum(sum_ref[...], axis=0)
     lower, inverse = load_factor(terms, fac_ref)
-    amp = solve(total, lower, inverse, cases, amp_ref)
+    amp = amplitudes_of(solve(total, lower, inverse, cases, amp_ref), cases)
     near = near_ref[...] + near_in[...]
     far = far_ref[...] + jnp.where((me == devices - 1), 0.0, far_in[...])
     live = mask_ref[0:1, width:]
     contact = mask_ref[1:2, width:] > 0.0
     open_part = jnp.where(live > 0.0, jnp.where(even, near, far), 0.0)
-    residual = open_part - project(amp, pieces_ref[:, width:], cases)
+    residual = open_part - dot(amp, stacked(pieces_ref[:, width:]))
+    res_out[...] = residual
+    res_copy = pltpu.make_async_copy(res_out, res_hbm, sems.at[0])
+    res_copy.start()
     update = chebyshev(residual, upd_ref[:, width:], rhos)
     mult = mult_ref[:, width:] + update
     mult_out[...] = jnp.where(contact, jnp.maximum(mult, 0.0), mult)
-    res_out[...] = residual
+    mult_copy = pltpu.make_async_copy(mult_out, mult_hbm, sems.at[1])
+    mult_copy.start()
     amp_out[...] = amp_ref[:terms, :cases]
+    res_copy.wait()
+    mult_copy.wait()
 
 
 def rows_of(count):
@@ -420,7 +448,7 @@
                 out_shape=shaped(*outputs),
                 in_specs=[VMEM] * len(inputs),
                 out_specs=[VMEM] * len(outputs),
-                scratch_shapes=amp_scratch,
+                scratch_shapes=amp_scratch + [pltpu.VMEM((cases, order), F32)],
                 compiler_params=params(12),
             )(*inputs)
             near, far, pay_out, mult, update = out[:5]
@@ -432,8 +460,10 @@
                 functools.partial(last_kernel, terms, rhos[step]),
                 out_shape=shaped(half, half, ((terms, cases), F32)),
                 in_specs=[VMEM] * len(inputs),
-                out_specs=[VMEM] * 3,
-                scratch_shapes=amp_scratch,
+                out_specs=[HBM, HBM, VMEM],
+                scratch_shapes=amp_scratch
+                + [pltpu.VMEM((cases, width), F32)] * 2
+                + [pltpu.SemaphoreType.DMA((2,))],
                 compiler_params=params(8),
                 name="last",
             )(*inputs)

time: 58.7 us -> 59.4 us (1.012)
  Pallas kernels: 7.94 us -> 8.62 us
    pallas_call x1, Pallas kernels: 1.08 us -> 1.68 us  [shards(): pl.pallas_call(functools.partial(last_kernel, terms, rhos[step]), out_sha...]
where the time goes in v3:
time: 59.4 us; the launch traced here: 59.2 us
  blocking collectives  35 us (59%)
  starting transfers between devices  8.92 us (15%)
  Pallas kernels  8.62 us (15%)
  waiting for transfers between devices  4.64 us (8%)
  between operations  2 us (3%)
    all_to_all x3, blocking collectives, shards(): gathered = lax.all_to_all(pay_out, AXES, 0, 0)  35 us
    ppermute x1, waiting for transfers between devices, shards(): halo = lax.ppermute(msg, AXES, ring)  4.62 us
    ppermute x3, starting transfers between devices, shards(): far_in = lax.ppermute(far, AXES, far_pairs)  4.13 us
    ppermute x1, starting transfers between devices, shards(): halo = lax.ppermute(msg, AXES, ring)  3.02 us
    pallas_call x2, Pallas kernels, shards(): pl.pallas_call(functools.partial(middle_kernel, terms, first, rhos[step])...  2.94 us
    pallas_call x1, Pallas kernels, shards(): pl.pallas_call(functools.partial(first_kernel, terms), out_shape=shaped((...  2.35 us
    ppermute x3, starting transfers between devices, shards(): near_in = lax.ppermute(near, AXES, near_pairs)  1.77 us
    pallas_call x1, Pallas kernels, shards(): pl.pallas_call(functools.partial(last_kernel, terms, rhos[step]), out_sha...  1.68 us
  transfers between devices with their start and end apart: 7, of which 1 were waited for; matrix products, arithmetic and copies ran while one was open for 0% of the time, Pallas kernels for 4%

profile of v3, /device:TPU:0, one launch (start us, length us, event | category | flops | bytes accessed | tf_op | source)
XLA Modules:
  0.0 59.2 jit_solution(12793879355182910845)
XLA Ops:
  1.9 0.9 %pack.1.msg_ref = f32[72,512]{1,0:T(8,128)S(1)} custom-call(s32[1]{0:T(128)S(6)} %copy.9.count_ref, s32[1]{0:T(128)S(6)} %copy.10.from_ref, f32[64,512]{1,0:T(8,128)} %bitcast.11, f32[6,1,512]{2,1,0:T(1,128)} %bitcast.12), custom_call_target="tpu_custom_call" | custom-call | tf_op jit(solution)/shard_map/pack/pallas_call | solution.py:385
  2.9 3.0 %collective-permute-start = (f32[72,512]{1,0:T(8,128)S(1)}, f32[72,512]{1,0:T(8,128)S(1)}, u32[]{:S(2)}, u32[]{:S(2)}) collective-permute-start(f32[72,512]{1,0:T(8,128)S(1)} %pack.1.msg_ref), channel_id=1, source_target_pairs={{0,1},{1,2},{2,3},{3,4},{4,5},{5,6},{6,7},{7,8},{8,9},{9,10},{10,1... | collective-permute-start | bytes 442376 | tf_op jit(solution)/shard_map/ppermute | solution.py:398
  5.9 0.0 copy-start
  5.9 2.4 %first.1 = (bf16[8,1024,128]{2,1,0:T(8,128)(2,1)S(1)}, bf16[8,1024,128]{2,1,0:T(8,128)(2,1)S(1)}, f32[64,1024]{1,0:T(8,128)S(1)}, f32[1,128]{1,0:T(1,128)S(1)}) custom-call(f32[1024,1024]{1,0:T(8,128)} %bitcast.10, f32[72,512]{1,0:T(8,128)S(1)} %pack.1.msg_ref), custom_call_target="tpu_custom_call" | custom-call | flops 268435456 | bytes 8388608 | tf_op jit(solution)/shard_map/first/pallas_call | solution.py:399
  8.3 4.6 %collective-permute-done.halo_ref = f32[72,512]{1,0:T(8,128)S(1)} collective-permute-done((f32[72,512]{1,0:T(8,128)S(1)}, f32[72,512]{1,0:T(8,128)S(1)}, u32[]{:S(2)}, u32[]{:S(2)}) %collective-permute-start) | collective-permute-done | bytes 147488 | tf_op jit(solution)/shard_map/ppermute | solution.py:398
  12.9 0.0 copy-done
  12.9 0.7 %second.1 = (f32[64,512]{1,0:T(8,128)S(1)}, f32[64,512]{1,0:T(8,128)S(1)}, f32[32,4,128]{2,1,0:T(4,128)S(1)}, f32[64,1024]{1,0:T(8,128)S(1)}, f32[2,1024]{1,0:T(2,128)S(1)}, /*index=5*/bf16[24,1024]{1,0:T(8,128)(2,1)S(1)}) custom-call(bf16[8,1024,128]{2,1,0:T(8,128)(2,1)S(1)} %get-tuple-element.27.high_ref, ...), custom_call_target="tpu_custom_call" | custom-call | tf_op jit(solution)/shard_map/second/pallas_call | solution.py:423
  13.6 0.1 collective-permute-start.1
  13.7 2.3 %collective-permute-start.2 = (f32[64,512]{1,0:T(8,128)S(1)}, f32[64,512]{1,0:T(8,128)S(1)}, u32[]{:S(2)}, u32[]{:S(2)}) collective-permute-start(f32[64,512]{1,0:T(8,128)S(1)} %get-tuple-element.33.far_ref), channel_id=1, source_target_pairs={{0,31},{1,2},{2,1},{3,4},{4,3},{5,6},{6,5},{7,8},{8,7},{9,10},{10,... | collective-permute-start | bytes 393224 | tf_op jit(solution)/shard_map/ppermute | solution.py:435
  16.0 11.3 %all_to_all.15.sum_ref = f32[32,4,128]{2,1,0:T(4,128)S(1)} all-to-all(f32[32,4,128]{2,1,0:T(4,128)S(1)} %get-tuple-element.31), channel_id=1, replica_groups=mesh['group'=4,'dev'=8] {'group','dev'}, dimensions={0} | all-to-all | bytes 131072 | tf_op jit(solution)/shard_map/all_to_all | solution.py:437
  27.3 0.0 collective-permute-done.1.near_in
  27.3 0.0 collective-permute-done.2.far_in
  27.3 1.5 %shard_map.85 = (f32[64,512]{1,0:T(8,128)S(1)}, f32[64,512]{1,0:T(8,128)S(1)}, f32[32,4,128]{2,1,0:T(4,128)S(1)}, f32[64,1024]{1,0:T(8,128)S(1)}, f32[64,1024]{1,0:T(8,128)S(1)}, /*index=5*/f32[24,128]{1,0:T(8,128)S(1)}) custom-call(f32[32,4,128]{2,1,0:T(4,128)S(1)} %all_to_all.15.sum_ref, f32[64,512]{1,0:T(8,128)S(1)} %get-tuple-element.32.near_ref, ...), custom_call_target="tpu_custom_call" | custom-call | tf_op jit(solution)/shard_map/pallas_call | solution.py:446
  28.8 0.8 %collective-permute-start.3 = (f32[64,512]{1,0:T(8,128)S(1)}, f32[64,512]{1,0:T(8,128)S(1)}, u32[]{:S(2)}, u32[]{:S(2)}) collective-permute-start(f32[64,512]{1,0:T(8,128)S(1)} %get-tuple-element.38.near_ref), channel_id=1, source_target_pairs={{0,1},{1,0},{2,3},{3,2},{4,5},{5,4},{6,7},{7,6},{8,9},{9,8},{10,11... | collective-permute-start | bytes 393224 | tf_op jit(solution)/shard_map/ppermute | solution.py:436
  29.7 0.9 %collective-permute-start.4 = (f32[64,512]{1,0:T(8,128)S(1)}, f32[64,512]{1,0:T(8,128)S(1)}, u32[]{:S(2)}, u32[]{:S(2)}) collective-permute-start(f32[64,512]{1,0:T(8,128)S(1)} %get-tuple-element.39.far_ref), channel_id=1, source_target_pairs={{0,31},{1,2},{2,1},{3,4},{4,3},{5,6},{6,5},{7,8},{8,7},{9,10},{10,... | collective-permute-start | bytes 393224 | tf_op jit(solution)/shard_map/ppermute | solution.py:435
  30.6 11.9 %all_to_all.16.sum_ref = f32[32,4,128]{2,1,0:T(4,128)S(1)} all-to-all(f32[32,4,128]{2,1,0:T(4,128)S(1)} %get-tuple-element.37), channel_id=1, replica_groups=mesh['group'=4,'dev'=8] {'group','dev'}, dimensions={0} | all-to-all | bytes 131072 | tf_op jit(solution)/shard_map/all_to_all | solution.py:437
  42.4 0.0 collective-permute-done.3.near_in
  42.4 0.0 collective-permute-done.4.far_in
  42.4 1.4 %shard_map.86 = (f32[64,512]{1,0:T(8,128)S(1)}, f32[64,512]{1,0:T(8,128)S(1)}, f32[32,4,128]{2,1,0:T(4,128)S(1)}, f32[64,1024]{1,0:T(8,128)S(1)}, f32[64,1024]{1,0:T(8,128)S(1)}) custom-call(f32[32,4,128]{2,1,0:T(4,128)S(1)} %all_to_all.16.sum_ref, f32[64,512]{1,0:T(8,128)S(1)} %get-tuple-element.38.near_ref, f32[64,512]{1,0:T(8,128)S(1)} %get-tuple-element.39.far_ref, ...), custom_call_target="tpu_custom_call" | custom-call | tf_op jit(solution)/shard_map/pallas_call | solution.py:446
  43.9 0.9 %collective-permute-start.5 = (f32[64,512]{1,0:T(8,128)S(1)}, f32[64,512]{1,0:T(8,128)S(1)}, u32[]{:S(2)}, u32[]{:S(2)}) collective-permute-start(f32[64,512]{1,0:T(8,128)S(1)} %get-tuple-element.44.near_ref), channel_id=1, source_target_pairs={{0,1},{1,0},{2,3},{3,2},{4,5},{5,4},{6,7},{7,6},{8,9},{9,8},{10,11... | collective-permute-start | bytes 393224 | tf_op jit(solution)/shard_map/ppermute | solution.py:436
  44.7 0.9 %collective-permute-start.6 = (f32[64,512]{1,0:T(8,128)S(1)}, f32[64,512]{1,0:T(8,128)S(1)}, u32[]{:S(2)}, u32[]{:S(2)}) collective-permute-start(f32[64,512]{1,0:T(8,128)S(1)} %get-tuple-element.45.far_ref), channel_id=1, source_target_pairs={{0,31},{1,2},{2,1},{3,4},{4,3},{5,6},{6,5},{7,8},{8,7},{9,10},{10,... | collective-permute-start | bytes 393224 | tf_op jit(solution)/shard_map/ppermute | solution.py:435
  45.7 11.9 %all_to_all.17.sum_ref = f32[32,4,128]{2,1,0:T(4,128)S(1)} all-to-all(f32[32,4,128]{2,1,0:T(4,128)S(1)} %get-tuple-element.43), channel_id=1, replica_groups=mesh['group'=4,'dev'=8] {'group','dev'}, dimensions={0} | all-to-all | bytes 131072 | tf_op jit(solution)/shard_map/all_to_all | solution.py:437
  57.5 0.0 collective-permute-done.5.near_in
  57.5 0.0 collective-permute-done.6.far_in
  57.5 1.7 %last.1 = (f32[64,512]{1,0:T(8,128)}, f32[64,512]{1,0:T(8,128)}, f32[6,64]{1,0:T(8,128)}) custom-call(f32[32,4,128]{2,1,0:T(4,128)S(1)} %all_to_all.17.sum_ref, f32[64,512]{1,0:T(8,128)S(1)} %get-tuple-element.44.near_ref, f32[64,512]{1,0:T(8,128)S(1)} %get-tuple-element.45.far_ref, f32[64,512]{1,0:T(8,128)S(1)} %collective-permute-done.5.near_in, ...), custom_call_target="tpu_custom_call" | custom-call | tf_op jit(solution)/shard_map/last/pallas_call | solution.py:459
Async XLA Ops:
  2.9 10.0 %collective-permute-start = (f32[72,512]{1,0:T(8,128)S(1)}, f32[72,512]{1,0:T(8,128)S(1)}, u32[]{:S(2)}, u32[]{:S(2)}) collective-permute-start(f32[72,512]{1,0:T(8,128)S(1)} %pack.1.msg_ref), channel_id=1, source_target_pairs={{0,1},{1,2},{2,3},{3,4},{4,5},{5,6},{6,7},{7,8},{8,9},{9,10},{10,1... | collective-permute-start | bytes 442376 | tf_op jit(solution)/shard_map/ppermute | solution.py:398
  5.9 7.0 %copy-start = (f32[1,64,512]{2,1,0:T(8,128)S(1)}, f32[1,64,512]{2,1,0:T(8,128)}, u32[]{:S(2)}) copy-start(f32[1,64,512]{2,1,0:T(8,128)} %param.8) | copy-start | bytes 393220
  13.6 13.7 %collective-permute-start.1 = (f32[64,512]{1,0:T(8,128)S(1)}, f32[64,512]{1,0:T(8,128)S(1)}, u32[]{:S(2)}, u32[]{:S(2)}) collective-permute-start(f32[64,512]{1,0:T(8,128)S(1)} %get-tuple-element.32.near_ref), channel_id=1, source_target_pairs={{0,1},{1,0},{2,3},{3,2},{4,5},{5,4},{6,7},{7,6},{8,9},{9,8},{10,11... | collective-permute-start | bytes 393224 | tf_op jit(solution)/shard_map/ppermute | solution.py:436
  13.7 13.6 %collective-permute-start.2 = (f32[64,512]{1,0:T(8,128)S(1)}, f32[64,512]{1,0:T(8,128)S(1)}, u32[]{:S(2)}, u32[]{:S(2)}) collective-permute-start(f32[64,512]{1,0:T(8,128)S(1)} %get-tuple-element.33.far_ref), channel_id=1, source_target_pairs={{0,31},{1,2},{2,1},{3,4},{4,3},{5,6},{6,5},{7,8},{8,7},{9,10},{10,... | collective-permute-start | bytes 393224 | tf_op jit(solution)/shard_map/ppermute | solution.py:435
  28.8 13.6 %collective-permute-start.3 = (f32[64,512]{1,0:T(8,128)S(1)}, f32[64,512]{1,0:T(8,128)S(1)}, u32[]{:S(2)}, u32[]{:S(2)}) collective-permute-start(f32[64,512]{1,0:T(8,128)S(1)} %get-tuple-element.38.near_ref), channel_id=1, source_target_pairs={{0,1},{1,0},{2,3},{3,2},{4,5},{5,4},{6,7},{7,6},{8,9},{9,8},{10,11... | collective-permute-start | bytes 393224 | tf_op jit(solution)/shard_map/ppermute | solution.py:436
  29.7 12.8 %collective-permute-start.4 = (f32[64,512]{1,0:T(8,128)S(1)}, f32[64,512]{1,0:T(8,128)S(1)}, u32[]{:S(2)}, u32[]{:S(2)}) collective-permute-start(f32[64,512]{1,0:T(8,128)S(1)} %get-tuple-element.39.far_ref), channel_id=1, source_target_pairs={{0,31},{1,2},{2,1},{3,4},{4,3},{5,6},{6,5},{7,8},{8,7},{9,10},{10,... | collective-permute-start | bytes 393224 | tf_op jit(solution)/shard_map/ppermute | solution.py:435
  43.9 13.6 %collective-permute-start.5 = (f32[64,512]{1,0:T(8,128)S(1)}, f32[64,512]{1,0:T(8,128)S(1)}, u32[]{:S(2)}, u32[]{:S(2)}) collective-permute-start(f32[64,512]{1,0:T(8,128)S(1)} %get-tuple-element.44.near_ref), channel_id=1, source_target_pairs={{0,1},{1,0},{2,3},{3,2},{4,5},{5,4},{6,7},{7,6},{8,9},{9,8},{10,11... | collective-permute-start | bytes 393224 | tf_op jit(solution)/shard_map/ppermute | solution.py:436
  44.7 12.8 %collective-permute-start.6 = (f32[64,512]{1,0:T(8,128)S(1)}, f32[64,512]{1,0:T(8,128)S(1)}, u32[]{:S(2)}, u32[]{:S(2)}) collective-permute-start(f32[64,512]{1,0:T(8,128)S(1)} %get-tuple-element.45.far_ref), channel_id=1, source_target_pairs={{0,31},{1,2},{2,1},{3,4},{4,3},{5,6},{6,5},{7,8},{8,7},{9,10},{10,... | collective-permute-start | bytes 393224 | tf_op jit(solution)/shard_map/ppermute | solution.py:435

commit v4 on v3

--- a/solution.py
+++ b/solution.py
@@ -148,8 +148,8 @@
                 cols = slice(n * WIDE - width, (n + 1) * WIDE - width)
                 partner = z[n - count // 2]
                 value = load_ref[:, cols] - value
-                near_ref[:, cols] = jnp.where(even, value, partner)
-                far_ref[:, cols] = jnp.where(even, partner, value)
+                near_ref[:, cols] = value if even is None else jnp.where(even, value, partner)
+                far_ref[:, cols] = partner if even is None else jnp.where(even, partner, value)
             z.append(value)
         if n >= LAG:
             part = pieces[:, (n - LAG) * WIDE : (n - LAG + 1) * WIDE]
@@ -272,7 +272,7 @@
 
 
 def middle_kernel(
-    terms, first, rhos, sum_ref, near_ref, far_ref, near_in, far_in, mult_ref, mask_ref, pieces_ref, load_ref,
+    terms, first, pairs, rhos, sum_ref, near_ref, far_ref, near_in, far_in, mult_ref, mask_ref, pieces_ref, load_ref,
     high_ref, low_ref, *rest,
 ):
     if first:
@@ -316,36 +316,28 @@
         return y[n] + block_product(both, high_ref, low_ref, start, n)
 
     no_gram = jnp.zeros((1, LANES), F32)
-    finish(block, terms, even, load_ref, pieces, no_gram, near_out, far_out, pay_ref)
+    finish(block, terms, even if pairs else None, load_ref, pieces, no_gram, near_out, far_out, pay_ref)
 
 
 def last_kernel(
-    terms, rhos, sum_ref, near_ref, far_ref, near_in, far_in, mult_ref, mask_ref, pieces_ref, upd_ref, fac_ref,
-    mult_hbm, res_hbm, amp_out, amp_ref, mult_out, res_out, sems,
+    terms, rhos, sum_ref, own_ref, next_in, mult_ref, mask_ref, pieces_ref, upd_ref, fac_ref,
+    mult_out, res_out, amp_out, amp_ref,
 ):
     cases, width = mult_out.shape
     me, devices = position()
-    even = me % 2 == 0
     total = jnp.sum(sum_ref[...], axis=0)
     lower, inverse = load_factor(terms, fac_ref)
     amp = amplitudes_of(solve(total, lower, inverse, cases, amp_ref), cases)
-    near = near_ref[...] + near_in[...]
-    far = far_ref[...] + jnp.where((me == devices - 1), 0.0, far_in[...])
+    open_part = own_ref[...] + jnp.where(me == devices - 1, 0.0, next_in[...])
     live = mask_ref[0:1, width:]
     contact = mask_ref[1:2, width:] > 0.0
-    open_part = jnp.where(live > 0.0, jnp.where(even, near, far), 0.0)
+    open_part = jnp.where(live > 0.0, open_part, 0.0)
     residual = open_part - dot(amp, stacked(pieces_ref[:, width:]))
     res_out[...] = residual
-    res_copy = pltpu.make_async_copy(res_out, res_hbm, sems.at[0])
-    res_copy.start()
     update = chebyshev(residual, upd_ref[:, width:], rhos)
     mult = mult_ref[:, width:] + update
     mult_out[...] = jnp.where(contact, jnp.maximum(mult, 0.0), mult)
-    mult_copy = pltpu.make_async_copy(mult_out, mult_hbm, sems.at[1])
-    mult_copy.start()
     amp_out[...] = amp_ref[:terms, :cases]
-    res_copy.wait()
-    mult_copy.wait()
 
 
 def rows_of(count):
@@ -372,6 +364,7 @@
     blocks = (order // LANES, order, LANES)
     slot = terms // (LANES // cases) + 1
     ring = [(i, (i + 1) % devices) for i in range(devices)]
+    back = [(target, source) for source, target in ring]
     near_pairs = [(i, i ^ 1) for i in range(devices)]
     far_pairs = [(i, (i + (1 if i % 2 else devices - 1)) % devices) for i in range(devices)]
 
@@ -432,8 +425,9 @@
     update = factor = None
     amp_scratch = [pltpu.VMEM((ROWS, LANES), F32)]
     for step in range(ITERS):
-        far_in = lax.ppermute(far, AXES, far_pairs)
-        near_in = lax.ppermute(near, AXES, near_pairs)
+        far_in = lax.ppermute(far, AXES, far_pairs if step < ITERS - 1 else back)
+        if step < ITERS - 1:
+            near_in = lax.ppermute(near, AXES, near_pairs)
         gathered = lax.all_to_all(pay_out, AXES, 0, 0)
         first = step == 0
         if step < ITERS - 1:
@@ -444,7 +438,7 @@
             else:
                 inputs += [update, factor]
             out = pl.pallas_call(
-                functools.partial(middle_kernel, terms, first, rhos[step]),
+                functools.partial(middle_kernel, terms, first, step < ITERS - 2, rhos[step]),
                 out_shape=shaped(*outputs),
                 in_specs=[VMEM] * len(inputs),
                 out_specs=[VMEM] * len(outputs),
@@ -455,15 +449,13 @@
             if first:
                 factor = out[5]
         else:
-            inputs = [gathered, near, far, near_in, far_in, mult, masks, pieces, update, factor]
+            inputs = [gathered, near, far_in, mult, masks, pieces, update, factor]
             mult, residual, amplitudes = pl.pallas_call(
                 functools.partial(last_kernel, terms, rhos[step]),
                 out_shape=shaped(half, half, ((terms, cases), F32)),
                 in_specs=[VMEM] * len(inputs),
-                out_specs=[HBM, HBM, VMEM],
-                scratch_shapes=amp_scratch
-                + [pltpu.VMEM((cases, width), F32)] * 2
-                + [pltpu.SemaphoreType.DMA((2,))],
+                out_specs=[VMEM] * 3,
+                scratch_shapes=amp_scratch,
                 compiler_params=params(8),
                 name="last",
             )(*inputs)

time: 59.4 us -> 55.3 us (0.931)
  blocking collectives: 35 us -> 32.5 us
  starting transfers between devices: 8.92 us -> 7.94 us
  Pallas kernels: 8.62 us -> 8 us
    all_to_all x3, blocking collectives: 35 us -> 32.5 us  [shards(): gathered = lax.all_to_all(pay_out, AXES, 0, 0)]
    ppermute x3 -> x2, starting transfers between devices: 1.77 us -> 0.92 us  [shards(): near_in = lax.ppermute(near, AXES, near_pairs)]
    pallas_call x1, Pallas kernels: 1.68 us -> 1.08 us  [shards(): pl.pallas_call(functools.partial(last_kernel, terms, rhos[step]), out_sha...]
  transfers between devices with their start and end apart: 7 -> 6, of which waited for: 1 -> 1; matrix products, arithmetic and copies ran while one was open for 0% -> 0% of each run, Pallas kernels for 4% -> 4%
where the time goes in v4:
time: 55.3 us; the launch traced here: 55 us
  blocking collectives  32.5 us (59%)
  Pallas kernels  8 us (14%)
  starting transfers between devices  7.94 us (14%)
  waiting for transfers between devices  4.63 us (8%)
  between operations  2.01 us (4%)
    all_to_all x3, blocking collectives, shards(): gathered = lax.all_to_all(pay_out, AXES, 0, 0)  32.5 us
    ppermute x1, waiting for transfers between devices, shards(): halo = lax.ppermute(msg, AXES, ring)  4.62 us
    ppermute x3, starting transfers between devices, shards(): far_in = lax.ppermute(far, AXES, far_pairs if step < ITERS - 1 else back)  4 us
    ppermute x1, starting transfers between devices, shards(): halo = lax.ppermute(msg, AXES, ring)  3.02 us
    pallas_call x2, Pallas kernels, shards(): pl.pallas_call(functools.partial(middle_kernel, terms, first, step < ITER...  2.92 us
    pallas_call x1, Pallas kernels, shards(): pl.pallas_call(functools.partial(first_kernel, terms), out_shape=shaped((...  2.35 us
  transfers between devices with their start and end apart: 6, of which 1 were waited for; matrix products, arithmetic and copies ran while one was open for 0% of the time, Pallas kernels for 4%

profile of v4, /device:TPU:0, one launch (start us, length us, event | category | flops | bytes accessed | tf_op | source)
XLA Modules:
  0.0 55.0 jit_solution(14697499420010239542)
XLA Ops:
  1.9 0.9 %pack.1.msg_ref = f32[72,512]{1,0:T(8,128)S(1)} custom-call(s32[1]{0:T(128)S(6)} %copy.9.count_ref, s32[1]{0:T(128)S(6)} %copy.10.from_ref, f32[64,512]{1,0:T(8,128)} %bitcast.11, f32[6,1,512]{2,1,0:T(1,128)} %bitcast.12), custom_call_target="tpu_custom_call" | custom-call | tf_op jit(solution)/shard_map/pack/pallas_call | solution.py:378
  2.9 3.0 %collective-permute-start = (f32[72,512]{1,0:T(8,128)S(1)}, f32[72,512]{1,0:T(8,128)S(1)}, u32[]{:S(2)}, u32[]{:S(2)}) collective-permute-start(f32[72,512]{1,0:T(8,128)S(1)} %pack.1.msg_ref), channel_id=1, source_target_pairs={{0,1},{1,2},{2,3},{3,4},{4,5},{5,6},{6,7},{7,8},{8,9},{9,10},{10,1... | collective-permute-start | bytes 442376 | tf_op jit(solution)/shard_map/ppermute | solution.py:391
  5.9 0.0 copy-start
  5.9 2.4 %first.1 = (bf16[8,1024,128]{2,1,0:T(8,128)(2,1)S(1)}, bf16[8,1024,128]{2,1,0:T(8,128)(2,1)S(1)}, f32[64,1024]{1,0:T(8,128)S(1)}, f32[1,128]{1,0:T(1,128)S(1)}) custom-call(f32[1024,1024]{1,0:T(8,128)} %bitcast.10, f32[72,512]{1,0:T(8,128)S(1)} %pack.1.msg_ref), custom_call_target="tpu_custom_call" | custom-call | flops 268435456 | bytes 8388608 | tf_op jit(solution)/shard_map/first/pallas_call | solution.py:392
  8.3 4.6 %collective-permute-done.halo_ref = f32[72,512]{1,0:T(8,128)S(1)} collective-permute-done((f32[72,512]{1,0:T(8,128)S(1)}, f32[72,512]{1,0:T(8,128)S(1)}, u32[]{:S(2)}, u32[]{:S(2)}) %collective-permute-start) | collective-permute-done | bytes 147488 | tf_op jit(solution)/shard_map/ppermute | solution.py:391
  12.9 0.0 copy-done
  12.9 0.7 %second.1 = (f32[64,512]{1,0:T(8,128)S(1)}, f32[64,512]{1,0:T(8,128)S(1)}, f32[32,4,128]{2,1,0:T(4,128)S(1)}, f32[64,1024]{1,0:T(8,128)S(1)}, f32[2,1024]{1,0:T(2,128)S(1)}, /*index=5*/bf16[24,1024]{1,0:T(8,128)(2,1)S(1)}) custom-call(bf16[8,1024,128]{2,1,0:T(8,128)(2,1)S(1)} %get-tuple-element.27.high_ref, ...), custom_call_target="tpu_custom_call" | custom-call | tf_op jit(solution)/shard_map/second/pallas_call | solution.py:416
  13.6 0.1 collective-permute-start.1
  13.7 2.3 %collective-permute-start.2 = (f32[64,512]{1,0:T(8,128)S(1)}, f32[64,512]{1,0:T(8,128)S(1)}, u32[]{:S(2)}, u32[]{:S(2)}) collective-permute-start(f32[64,512]{1,0:T(8,128)S(1)} %get-tuple-element.33.far_ref), channel_id=1, source_target_pairs={{0,31},{1,2},{2,1},{3,4},{4,3},{5,6},{6,5},{7,8},{8,7},{9,10},{10,... | collective-permute-start | bytes 393224 | tf_op jit(solution)/shard_map/ppermute | solution.py:428
  16.0 11.3 %all_to_all.15.sum_ref = f32[32,4,128]{2,1,0:T(4,128)S(1)} all-to-all(f32[32,4,128]{2,1,0:T(4,128)S(1)} %get-tuple-element.31), channel_id=1, replica_groups=mesh['group'=4,'dev'=8] {'group','dev'}, dimensions={0} | all-to-all | bytes 131072 | tf_op jit(solution)/shard_map/all_to_all | solution.py:431
  27.3 0.0 collective-permute-done.1.near_in
  27.3 0.0 collective-permute-done.2.far_in
  27.3 1.5 %shard_map.85 = (f32[64,512]{1,0:T(8,128)S(1)}, f32[64,512]{1,0:T(8,128)S(1)}, f32[32,4,128]{2,1,0:T(4,128)S(1)}, f32[64,1024]{1,0:T(8,128)S(1)}, f32[64,1024]{1,0:T(8,128)S(1)}, /*index=5*/f32[24,128]{1,0:T(8,128)S(1)}) custom-call(f32[32,4,128]{2,1,0:T(4,128)S(1)} %all_to_all.15.sum_ref, f32[64,512]{1,0:T(8,128)S(1)} %get-tuple-element.32.near_ref, ...), custom_call_target="tpu_custom_call" | custom-call | tf_op jit(solution)/shard_map/pallas_call | solution.py:440
  28.8 0.8 %collective-permute-start.3 = (f32[64,512]{1,0:T(8,128)S(1)}, f32[64,512]{1,0:T(8,128)S(1)}, u32[]{:S(2)}, u32[]{:S(2)}) collective-permute-start(f32[64,512]{1,0:T(8,128)S(1)} %get-tuple-element.38.near_ref), channel_id=1, source_target_pairs={{0,1},{1,0},{2,3},{3,2},{4,5},{5,4},{6,7},{7,6},{8,9},{9,8},{10,11... | collective-permute-start | bytes 393224 | tf_op jit(solution)/shard_map/ppermute | solution.py:430
  29.7 0.9 %collective-permute-start.4 = (f32[64,512]{1,0:T(8,128)S(1)}, f32[64,512]{1,0:T(8,128)S(1)}, u32[]{:S(2)}, u32[]{:S(2)}) collective-permute-start(f32[64,512]{1,0:T(8,128)S(1)} %get-tuple-element.39.far_ref), channel_id=1, source_target_pairs={{0,31},{1,2},{2,1},{3,4},{4,3},{5,6},{6,5},{7,8},{8,7},{9,10},{10,... | collective-permute-start | bytes 393224 | tf_op jit(solution)/shard_map/ppermute | solution.py:428
  30.6 11.9 %all_to_all.16.sum_ref = f32[32,4,128]{2,1,0:T(4,128)S(1)} all-to-all(f32[32,4,128]{2,1,0:T(4,128)S(1)} %get-tuple-element.37), channel_id=1, replica_groups=mesh['group'=4,'dev'=8] {'group','dev'}, dimensions={0} | all-to-all | bytes 131072 | tf_op jit(solution)/shard_map/all_to_all | solution.py:431
  42.4 0.0 collective-permute-done.3.near_in
  42.4 0.0 collective-permute-done.4.far_in
  42.4 1.4 %shard_map.86 = (f32[64,512]{1,0:T(8,128)S(1)}, f32[64,512]{1,0:T(8,128)S(1)}, f32[32,4,128]{2,1,0:T(4,128)S(1)}, f32[64,1024]{1,0:T(8,128)S(1)}, f32[64,1024]{1,0:T(8,128)S(1)}) custom-call(f32[32,4,128]{2,1,0:T(4,128)S(1)} %all_to_all.16.sum_ref, f32[64,512]{1,0:T(8,128)S(1)} %get-tuple-element.38.near_ref, f32[64,512]{1,0:T(8,128)S(1)} %get-tuple-element.39.far_ref, ...), custom_call_target="tpu_custom_call" | custom-call | tf_op jit(solution)/shard_map/pallas_call | solution.py:440
  43.9 0.8 %collective-permute-start.5 = (f32[64,512]{1,0:T(8,128)S(1)}, f32[64,512]{1,0:T(8,128)S(1)}, u32[]{:S(2)}, u32[]{:S(2)}) collective-permute-start(f32[64,512]{1,0:T(8,128)S(1)} %get-tuple-element.45), channel_id=1, source_target_pairs={{1,0},{2,1},{3,2},{4,3},{5,4},{6,5},{7,6},{8,7},{9,8},{10,9},{11,1... | collective-permute-start | bytes 393224 | tf_op jit(solution)/shard_map/ppermute | solution.py:428
  44.7 9.3 %all_to_all.17.sum_ref = f32[32,4,128]{2,1,0:T(4,128)S(1)} all-to-all(f32[32,4,128]{2,1,0:T(4,128)S(1)} %get-tuple-element.43), channel_id=1, replica_groups=mesh['group'=4,'dev'=8] {'group','dev'}, dimensions={0} | all-to-all | bytes 131072 | tf_op jit(solution)/shard_map/all_to_all | solution.py:431
  54.0 0.0 collective-permute-done.5.next_in
  54.0 1.1 %last.1 = (f32[64,512]{1,0:T(8,128)}, f32[64,512]{1,0:T(8,128)}, f32[6,64]{1,0:T(8,128)}) custom-call(f32[32,4,128]{2,1,0:T(4,128)S(1)} %all_to_all.17.sum_ref, f32[64,512]{1,0:T(8,128)S(1)} %get-tuple-element.44.own_ref, f32[64,512]{1,0:T(8,128)S(1)} %collective-permute-done.5.next_in, f32[64,1024]{1,0:T(8,128)S(1)} %get-tuple-element.46.mult_ref, ...), custom_call_target="tpu_custom_call" | custom-call | tf_op jit(solution)/shard_map/last/pallas_call | solution.py:453
Async XLA Ops:
  2.9 10.0 %collective-permute-start = (f32[72,512]{1,0:T(8,128)S(1)}, f32[72,512]{1,0:T(8,128)S(1)}, u32[]{:S(2)}, u32[]{:S(2)}) collective-permute-start(f32[72,512]{1,0:T(8,128)S(1)} %pack.1.msg_ref), channel_id=1, source_target_pairs={{0,1},{1,2},{2,3},{3,4},{4,5},{5,6},{6,7},{7,8},{8,9},{9,10},{10,1... | collective-permute-start | bytes 442376 | tf_op jit(solution)/shard_map/ppermute | solution.py:391
  5.9 7.0 %copy-start = (f32[1,64,512]{2,1,0:T(8,128)S(1)}, f32[1,64,512]{2,1,0:T(8,128)}, u32[]{:S(2)}) copy-start(f32[1,64,512]{2,1,0:T(8,128)} %param.8) | copy-start | bytes 393220
  13.6 13.7 %collective-permute-start.1 = (f32[64,512]{1,0:T(8,128)S(1)}, f32[64,512]{1,0:T(8,128)S(1)}, u32[]{:S(2)}, u32[]{:S(2)}) collective-permute-start(f32[64,512]{1,0:T(8,128)S(1)} %get-tuple-element.32.near_ref), channel_id=1, source_target_pairs={{0,1},{1,0},{2,3},{3,2},{4,5},{5,4},{6,7},{7,6},{8,9},{9,8},{10,11... | collective-permute-start | bytes 393224 | tf_op jit(solution)/shard_map/ppermute | solution.py:430
  13.7 13.6 %collective-permute-start.2 = (f32[64,512]{1,0:T(8,128)S(1)}, f32[64,512]{1,0:T(8,128)S(1)}, u32[]{:S(2)}, u32[]{:S(2)}) collective-permute-start(f32[64,512]{1,0:T(8,128)S(1)} %get-tuple-element.33.far_ref), channel_id=1, source_target_pairs={{0,31},{1,2},{2,1},{3,4},{4,3},{5,6},{6,5},{7,8},{8,7},{9,10},{10,... | collective-permute-start | bytes 393224 | tf_op jit(solution)/shard_map/ppermute | solution.py:428
  28.8 13.6 %collective-permute-start.3 = (f32[64,512]{1,0:T(8,128)S(1)}, f32[64,512]{1,0:T(8,128)S(1)}, u32[]{:S(2)}, u32[]{:S(2)}) collective-permute-start(f32[64,512]{1,0:T(8,128)S(1)} %get-tuple-element.38.near_ref), channel_id=1, source_target_pairs={{0,1},{1,0},{2,3},{3,2},{4,5},{5,4},{6,7},{7,6},{8,9},{9,8},{10,11... | collective-permute-start | bytes 393224 | tf_op jit(solution)/shard_map/ppermute | solution.py:430
  29.7 12.8 %collective-permute-start.4 = (f32[64,512]{1,0:T(8,128)S(1)}, f32[64,512]{1,0:T(8,128)S(1)}, u32[]{:S(2)}, u32[]{:S(2)}) collective-permute-start(f32[64,512]{1,0:T(8,128)S(1)} %get-tuple-element.39.far_ref), channel_id=1, source_target_pairs={{0,31},{1,2},{2,1},{3,4},{4,3},{5,6},{6,5},{7,8},{8,7},{9,10},{10,... | collective-permute-start | bytes 393224 | tf_op jit(solution)/shard_map/ppermute | solution.py:428
  43.9 10.1 %collective-permute-start.5 = (f32[64,512]{1,0:T(8,128)S(1)}, f32[64,512]{1,0:T(8,128)S(1)}, u32[]{:S(2)}, u32[]{:S(2)}) collective-permute-start(f32[64,512]{1,0:T(8,128)S(1)} %get-tuple-element.45), channel_id=1, source_target_pairs={{1,0},{2,1},{3,2},{4,3},{5,4},{6,5},{7,6},{8,7},{9,8},{10,9},{11,1... | collective-permute-start | bytes 393224 | tf_op jit(solution)/shard_map/ppermute | solution.py:428

commit v5 on v4

--- a/solution.py
+++ b/solution.py
@@ -70,34 +70,33 @@
     return me, lax.axis_size("group") * lax.axis_size("dev")
 
 
-def pack_kernel(count_ref, from_ref, warm_hbm, modes_hbm, out_ref, warm_ref, modes_ref, sems):
+def pack_kernel(count_ref, from_ref, warm_hbm, modes_hbm, out_ref, tail_ref, warm_ref, modes_ref, sems):
     copies = [
         pltpu.make_async_copy(source, target, sems.at[n])
         for n, (source, target) in enumerate(((warm_hbm, warm_ref), (modes_hbm, modes_ref)))
     ]
     for copy in copies:
         copy.start()
-    cases, width = warm_ref.shape
+    _, width = warm_ref.shape
     terms = modes_ref.shape[0]
-    spare = out_ref.shape[0] - cases - terms
+    spare = tail_ref.shape[0] - terms
     dofs = lax.broadcasted_iota(jnp.int32, (1, width), 1)
     alive = dofs < count_ref[0] * BLK
     live = alive.astype(F32)
     contact = (alive & (dofs >= from_ref[0])).astype(F32)
     for copy in copies:
         copy.wait()
-    out_ref[:cases, :] = warm_ref[...] * live
+    out_ref[...] = warm_ref[...] * live
     for c in range(terms):
-        out_ref[cases + c : cases + c + 1, :] = modes_ref[c] * live
+        tail_ref[c : c + 1, :] = modes_ref[c] * live
     if spare > 2:
-        out_ref[cases + terms :, :] = jnp.zeros((spare, width), F32)
-    out_ref[-2:-1, :] = live
-    out_ref[-1:, :] = contact
-
-
-def first_kernel(terms, schur_ref, msg_ref, high_ref, low_ref, own_ref, gram_ref, raw, acc, wide, sems):
+        tail_ref[terms:, :] = jnp.zeros((spare, width), F32)
+    tail_ref[-2:-1, :] = live
+    tail_ref[-1:, :] = contact
+
+
+def first_kernel(terms, schur_ref, msg_ref, tail_ref, high_ref, low_ref, own_ref, gram_ref, raw, acc, wide, sems):
     order = schur_ref.shape[0]
-    cases = own_ref.shape[0]
     chunks = order // CHUNK
     half = chunks // 2
     sequence = list(range(half, chunks)) + list(range(half))
@@ -108,7 +107,7 @@
 
     for c in sequence:
         copy(c).start()
-    modes = msg_ref[cases : cases + ROWS, :]
+    modes = tail_ref[:ROWS, :]
     modes = jnp.where(lax.broadcasted_iota(jnp.int32, modes.shape, 0) < terms, modes, 0.0)
     wide[...] = jnp.zeros_like(wide)
     wide[:, :ROWS] = lax.dot_general(
@@ -127,7 +126,7 @@
             high_ref[j, c * CHUNK : (c + 1) * CHUNK, :] = high[:, lanes]
             low_ref[j, c * CHUNK : (c + 1) * CHUNK, :] = low[:, lanes]
         if n < half:
-            part = product(msg_ref[:cases, n * CHUNK : (n + 1) * CHUNK], high, low)
+            part = product(msg_ref[:, n * CHUNK : (n + 1) * CHUNK], high, low)
             if n == 0:
                 acc[...] = part
             else:
@@ -166,16 +165,14 @@
 
 
 def second_kernel(
-    terms, high_ref, low_ref, own_ref, halo_ref, msg_ref, load_ref, gram_ref,
+    terms, high_ref, low_ref, own_ref, halo_ref, halo_tail_ref, msg_ref, tail_ref, load_ref, gram_ref,
     near_ref, far_ref, pay_ref, mult_ref, mask_ref, pieces_ref,
 ):
-    cases, _ = load_ref.shape
     me, _ = position()
-    halo = jnp.where(me > 0, halo_ref[...], 0.0)
-    left = halo[:cases]
-    tail = halo_ref.shape[0] - 2
-    mask_ref[0:2, :] = jnp.concatenate([halo[tail:], msg_ref[tail:, :]], axis=1)
-    modes = jnp.concatenate([halo[cases : cases + ROWS], msg_ref[cases : cases + ROWS, :]], axis=1)
+    halo_tail = jnp.where(me > 0, halo_tail_ref[...], 0.0)
+    left = jnp.where(halo_tail[-2:-1] > 0.0, halo_ref[...], 0.0)
+    mask_ref[...] = jnp.concatenate([halo_tail[-2:], tail_ref[-2:, :]], axis=1)
+    modes = jnp.concatenate([halo_tail[:ROWS], tail_ref[:ROWS, :]], axis=1)
     modes = jnp.where(lax.broadcasted_iota(jnp.int32, modes.shape, 0) < terms, modes, 0.0)
     pieces = jnp.concatenate(split3(modes), axis=0)
     pieces_ref[...] = pieces
@@ -185,7 +182,7 @@
         return own_ref[:, n * WIDE : (n + 1) * WIDE] - block_product(both, high_ref, low_ref, 0, n)
 
     finish(block, terms, me % 2 == 0, load_ref, pieces, gram_ref[...], near_ref, far_ref, pay_ref)
-    mult_ref[...] = jnp.concatenate([left, msg_ref[:cases, :]], axis=1)
+    mult_ref[...] = jnp.concatenate([left, msg_ref[...]], axis=1)
 
 
 def factor_rows(row, terms):
@@ -375,11 +372,12 @@
         rhos.append((rho, rho_new))
         rho = rho_new
 
-    msg = pl.pallas_call(
+    halo = lax.ppermute(warm_start[0], AXES, ring)
+    msg, tail = pl.pallas_call(
         pack_kernel,
-        out_shape=jax.ShapeDtypeStruct((rows_of(cases + terms + 2), width), F32),
+        out_shape=shaped(((cases, width), F32), ((rows_of(terms + 2), width), F32)),
         in_specs=[SMEM, SMEM, HBM, HBM],
-        out_specs=VMEM,
+        out_specs=[VMEM] * 2,
         scratch_shapes=[
             pltpu.VMEM((cases, width), F32),
             pltpu.VMEM((terms, 1, width), F32),
@@ -388,13 +386,13 @@
         compiler_params=params(4),
         name="pack",
     )(active_blocks, contact_from, in_hbm(warm_start[0]), in_hbm(jnp.transpose(coarse_modes, (1, 0, 2))))
-    halo = lax.ppermute(msg, AXES, ring)
+    halo_tail = lax.ppermute(tail, AXES, ring)
     high, low, own, gram_row = pl.pallas_call(
         functools.partial(first_kernel, terms),
         out_shape=shaped(
             (blocks, BF16), (blocks, BF16), ((cases, order), F32), ((1, LANES), F32)
         ),
-        in_specs=[HBM, VMEM],
+        in_specs=[HBM, VMEM, VMEM],
         out_specs=[VMEM] * 4,
         scratch_shapes=[
             pltpu.VMEM((order, order), F32),
@@ -407,7 +405,7 @@
             flops=4 * cases * order * order, bytes_accessed=8 * order * order, transcendentals=0
         ),
         name="first",
-    )(in_hbm(schur[0]), msg)
+    )(in_hbm(schur[0]), msg, tail)
 
     half = ((cases, width), F32)
     full = ((cases, order), F32)
@@ -416,11 +414,11 @@
     near, far, pay_out, mult, masks, pieces = pl.pallas_call(
         functools.partial(second_kernel, terms),
         out_shape=shaped(half, half, payload, full, ((2, order), F32), ((3 * ROWS, order), BF16)),
-        in_specs=[VMEM] * 7,
+        in_specs=[VMEM] * 9,
         out_specs=[VMEM] * 6,
         compiler_params=params(8),
         name="second",
-    )(high, low, own, halo, msg, load[0], gram_row)
+    )(high, low, own, halo, halo_tail, msg, tail, load[0], gram_row)
 
     update = factor = None
     amp_scratch = [pltpu.VMEM((ROWS, LANES), F32)]

time: 55.3 us -> 54.4 us (0.984)
  waiting for transfers between devices: 4.63 us -> 2.87 us
  starting transfers between devices: 7.94 us -> 8.84 us
    ppermute x1 -> x2, waiting for transfers between devices: 4.62 us -> 2.85 us  [the longest x1 2.85 us: shards(): halo_tail = lax.ppermute(tail, AXES, ring)]
    ppermute x1 -> x2, starting transfers between devices: 3.02 us -> 4.63 us  [the longest x1 3.02 us: shards(): halo = lax.ppermute(warm_start[0], AXES, ring)]
    ppermute x3, starting transfers between devices: 4 us -> 3.29 us  [shards(): far_in = lax.ppermute(far, AXES, far_pairs if step < ITERS - 1 else back)]
  transfers between devices with their start and end apart: 6 -> 7, of which waited for: 1 -> 1; matrix products, arithmetic and copies ran while one was open for 0% -> 0% of each run, Pallas kernels for 4% -> 6%
where the time goes in v5:
time: 54.4 us; the launch traced here: 54.2 us
  blocking collectives  32.5 us (60%)
  starting transfers between devices  8.84 us (16%)
  Pallas kernels  8 us (15%)
  waiting for transfers between devices  2.87 us (5%)
  between operations  2.02 us (4%)
    all_to_all x3, blocking collectives, shards(): gathered = lax.all_to_all(pay_out, AXES, 0, 0)  32.5 us
    ppermute x3, starting transfers between devices, shards(): far_in = lax.ppermute(far, AXES, far_pairs if step < ITERS - 1 else back)  3.29 us
    ppermute x1, starting transfers between devices, shards(): halo = lax.ppermute(warm_start[0], AXES, ring)  3.02 us
    pallas_call x2, Pallas kernels, shards(): pl.pallas_call(functools.partial(middle_kernel, terms, first, step < ITER...  2.92 us
    ppermute x1, waiting for transfers between devices, shards(): halo_tail = lax.ppermute(tail, AXES, ring)  2.85 us
    pallas_call x1, Pallas kernels, shards(): pl.pallas_call(functools.partial(first_kernel, terms), out_shape=shaped((...  2.35 us
    ppermute x1, starting transfers between devices, shards(): halo_tail = lax.ppermute(tail, AXES, ring)  1.61 us
  transfers between devices with their start and end apart: 7, of which 1 were waited for; matrix products, arithmetic and copies ran while one was open for 0% of the time, Pallas kernels for 6%

profile of v5, /device:TPU:0, one launch (start us, length us, event | category | flops | bytes accessed | tf_op | source)
XLA Modules:
  0.0 54.2 jit_solution(14609986777950255281)
XLA Ops:
  0.6 3.0 %collective-permute-start = (f32[64,512]{1,0:T(8,128)}, f32[64,512]{1,0:T(8,128)S(1)}, u32[]{:S(2)}, u32[]{:S(2)}) collective-permute-start(f32[64,512]{1,0:T(8,128)} %bitcast.11), channel_id=1, source_target_pairs={{0,1},{1,2},{2,3},{3,4},{4,5},{5,6},{6,7},{7,8},{8,9},{9,10},{10,1... | collective-permute-start | bytes 393224 | tf_op jit(solution)/shard_map/ppermute | solution.py:375
  5.0 0.9 %pack.1 = (f32[64,512]{1,0:T(8,128)S(1)}, f32[8,512]{1,0:T(8,128)S(1)}) custom-call(s32[1]{0:T(128)S(6)} %copy.9.count_ref, s32[1]{0:T(128)S(6)} %copy.10.from_ref, f32[64,512]{1,0:T(8,128)} %bitcast.12, f32[6,1,512]{2,1,0:T(1,128)} %bitcast.13), custom_call_target="tpu_custom_call" | custom-call | tf_op jit(solution)/shard_map/pack/pallas_call | solution.py:376
  5.9 1.6 %collective-permute-start.1 = (f32[8,512]{1,0:T(8,128)S(1)}, f32[8,512]{1,0:T(8,128)S(1)}, u32[]{:S(2)}, u32[]{:S(2)}) collective-permute-start(f32[8,512]{1,0:T(8,128)S(1)} %get-tuple-element.30.tail_ref), channel_id=1, source_target_pairs={{0,1},{1,2},{2,3},{3,4},{4,5},{5,6},{6,7},{7,8},{8,9},{9,10},{10,1... | collective-permute-start | bytes 49160 | tf_op jit(solution)/shard_map/ppermute | solution.py:389
  7.5 0.0 copy-start
  7.5 2.4 %first.1 = (bf16[8,1024,128]{2,1,0:T(8,128)(2,1)S(1)}, bf16[8,1024,128]{2,1,0:T(8,128)(2,1)S(1)}, f32[64,1024]{1,0:T(8,128)S(1)}, f32[1,128]{1,0:T(1,128)S(1)}) custom-call(f32[1024,1024]{1,0:T(8,128)} %bitcast.10, f32[64,512]{1,0:T(8,128)S(1)} %get-tuple-element.29.msg_ref, f32[8,512]{1,0:T(8,128)S(1)} %get-tuple-element.30.tail_ref), custom_call_target="tpu_custom_call" | custom-call | flops 268435456 | bytes 8388608 | tf_op jit(solution)/shard_map/first/pallas_call | solution.py:390
  9.9 2.8 %collective-permute-done.1.halo_tail_ref = f32[8,512]{1,0:T(8,128)S(1)} collective-permute-done((f32[8,512]{1,0:T(8,128)S(1)}, f32[8,512]{1,0:T(8,128)S(1)}, u32[]{:S(2)}, u32[]{:S(2)}) %collective-permute-start.1) | collective-permute-done | bytes 16416 | tf_op jit(solution)/shard_map/ppermute | solution.py:389
  12.7 0.0 collective-permute-done.halo_ref
  12.7 0.0 copy-done
  12.7 0.7 %second.1 = (f32[64,512]{1,0:T(8,128)S(1)}, f32[64,512]{1,0:T(8,128)S(1)}, f32[32,4,128]{2,1,0:T(4,128)S(1)}, f32[64,1024]{1,0:T(8,128)S(1)}, f32[2,1024]{1,0:T(2,128)S(1)}, /*index=5*/bf16[24,1024]{1,0:T(8,128)(2,1)S(1)}) custom-call(bf16[8,1024,128]{2,1,0:T(8,128)(2,1)S(1)} %get-tuple-element.31.high_ref, ...), custom_call_target="tpu_custom_call" | custom-call | tf_op jit(solution)/shard_map/second/pallas_call | solution.py:414
  13.4 0.1 collective-permute-start.2
  13.5 1.6 %collective-permute-start.3 = (f32[64,512]{1,0:T(8,128)S(1)}, f32[64,512]{1,0:T(8,128)S(1)}, u32[]{:S(2)}, u32[]{:S(2)}) collective-permute-start(f32[64,512]{1,0:T(8,128)S(1)} %get-tuple-element.37.far_ref), channel_id=1, source_target_pairs={{0,31},{1,2},{2,1},{3,4},{4,3},{5,6},{6,5},{7,8},{8,7},{9,10},{10,... | collective-permute-start | bytes 393224 | tf_op jit(solution)/shard_map/ppermute | solution.py:426
  15.1 11.3 %all_to_all.15.sum_ref = f32[32,4,128]{2,1,0:T(4,128)S(1)} all-to-all(f32[32,4,128]{2,1,0:T(4,128)S(1)} %get-tuple-element.35), channel_id=1, replica_groups=mesh['group'=4,'dev'=8] {'group','dev'}, dimensions={0} | all-to-all | bytes 131072 | tf_op jit(solution)/shard_map/all_to_all | solution.py:429
  26.4 0.0 collective-permute-done.2.near_in
  26.4 0.0 collective-permute-done.3.far_in
  26.4 1.5 %shard_map.85 = (f32[64,512]{1,0:T(8,128)S(1)}, f32[64,512]{1,0:T(8,128)S(1)}, f32[32,4,128]{2,1,0:T(4,128)S(1)}, f32[64,1024]{1,0:T(8,128)S(1)}, f32[64,1024]{1,0:T(8,128)S(1)}, /*index=5*/f32[24,128]{1,0:T(8,128)S(1)}) custom-call(f32[32,4,128]{2,1,0:T(4,128)S(1)} %all_to_all.15.sum_ref, f32[64,512]{1,0:T(8,128)S(1)} %get-tuple-element.36.near_ref, ...), custom_call_target="tpu_custom_call" | custom-call | tf_op jit(solution)/shard_map/pallas_call | solution.py:438
  28.0 0.8 %collective-permute-start.4 = (f32[64,512]{1,0:T(8,128)S(1)}, f32[64,512]{1,0:T(8,128)S(1)}, u32[]{:S(2)}, u32[]{:S(2)}) collective-permute-start(f32[64,512]{1,0:T(8,128)S(1)} %get-tuple-element.42.near_ref), channel_id=1, source_target_pairs={{0,1},{1,0},{2,3},{3,2},{4,5},{5,4},{6,7},{7,6},{8,9},{9,8},{10,11... | collective-permute-start | bytes 393224 | tf_op jit(solution)/shard_map/ppermute | solution.py:428
  28.8 0.9 %collective-permute-start.5 = (f32[64,512]{1,0:T(8,128)S(1)}, f32[64,512]{1,0:T(8,128)S(1)}, u32[]{:S(2)}, u32[]{:S(2)}) collective-permute-start(f32[64,512]{1,0:T(8,128)S(1)} %get-tuple-element.43.far_ref), channel_id=1, source_target_pairs={{0,31},{1,2},{2,1},{3,4},{4,3},{5,6},{6,5},{7,8},{8,7},{9,10},{10,... | collective-permute-start | bytes 393224 | tf_op jit(solution)/shard_map/ppermute | solution.py:426
  29.7 11.9 %all_to_all.16.sum_ref = f32[32,4,128]{2,1,0:T(4,128)S(1)} all-to-all(f32[32,4,128]{2,1,0:T(4,128)S(1)} %get-tuple-element.41), channel_id=1, replica_groups=mesh['group'=4,'dev'=8] {'group','dev'}, dimensions={0} | all-to-all | bytes 131072 | tf_op jit(solution)/shard_map/all_to_all | solution.py:429
  41.6 0.0 collective-permute-done.4.near_in
  41.6 0.0 collective-permute-done.5.far_in
  41.6 1.4 %shard_map.86 = (f32[64,512]{1,0:T(8,128)S(1)}, f32[64,512]{1,0:T(8,128)S(1)}, f32[32,4,128]{2,1,0:T(4,128)S(1)}, f32[64,1024]{1,0:T(8,128)S(1)}, f32[64,1024]{1,0:T(8,128)S(1)}) custom-call(f32[32,4,128]{2,1,0:T(4,128)S(1)} %all_to_all.16.sum_ref, f32[64,512]{1,0:T(8,128)S(1)} %get-tuple-element.42.near_ref, f32[64,512]{1,0:T(8,128)S(1)} %get-tuple-element.43.far_ref, ...), custom_call_target="tpu_custom_call" | custom-call | tf_op jit(solution)/shard_map/pallas_call | solution.py:438
  43.0 0.8 %collective-permute-start.6 = (f32[64,512]{1,0:T(8,128)S(1)}, f32[64,512]{1,0:T(8,128)S(1)}, u32[]{:S(2)}, u32[]{:S(2)}) collective-permute-start(f32[64,512]{1,0:T(8,128)S(1)} %get-tuple-element.49), channel_id=1, source_target_pairs={{1,0},{2,1},{3,2},{4,3},{5,4},{6,5},{7,6},{8,7},{9,8},{10,9},{11,1... | collective-permute-start | bytes 393224 | tf_op jit(solution)/shard_map/ppermute | solution.py:426
  43.8 9.3 %all_to_all.17.sum_ref = f32[32,4,128]{2,1,0:T(4,128)S(1)} all-to-all(f32[32,4,128]{2,1,0:T(4,128)S(1)} %get-tuple-element.47), channel_id=1, replica_groups=mesh['group'=4,'dev'=8] {'group','dev'}, dimensions={0} | all-to-all | bytes 131072 | tf_op jit(solution)/shard_map/all_to_all | solution.py:429
  53.1 0.0 collective-permute-done.6.next_in
  53.1 1.1 %last.1 = (f32[64,512]{1,0:T(8,128)}, f32[64,512]{1,0:T(8,128)}, f32[6,64]{1,0:T(8,128)}) custom-call(f32[32,4,128]{2,1,0:T(4,128)S(1)} %all_to_all.17.sum_ref, f32[64,512]{1,0:T(8,128)S(1)} %get-tuple-element.48.own_ref, f32[64,512]{1,0:T(8,128)S(1)} %collective-permute-done.6.next_in, f32[64,1024]{1,0:T(8,128)S(1)} %get-tuple-element.50.mult_ref, ...), custom_call_target="tpu_custom_call" | custom-call | tf_op jit(solution)/shard_map/last/pallas_call | solution.py:451
Async XLA Ops:
  0.6 12.1 %collective-permute-start = (f32[64,512]{1,0:T(8,128)}, f32[64,512]{1,0:T(8,128)S(1)}, u32[]{:S(2)}, u32[]{:S(2)}) collective-permute-start(f32[64,512]{1,0:T(8,128)} %bitcast.11), channel_id=1, source_target_pairs={{0,1},{1,2},{2,3},{3,4},{4,5},{5,6},{6,7},{7,8},{8,9},{9,10},{10,1... | collective-permute-start | bytes 393224 | tf_op jit(solution)/shard_map/ppermute | solution.py:375
  5.9 6.8 %collective-permute-start.1 = (f32[8,512]{1,0:T(8,128)S(1)}, f32[8,512]{1,0:T(8,128)S(1)}, u32[]{:S(2)}, u32[]{:S(2)}) collective-permute-start(f32[8,512]{1,0:T(8,128)S(1)} %get-tuple-element.30.tail_ref), channel_id=1, source_target_pairs={{0,1},{1,2},{2,3},{3,4},{4,5},{5,6},{6,7},{7,8},{8,9},{9,10},{10,1... | collective-permute-start | bytes 49160 | tf_op jit(solution)/shard_map/ppermute | solution.py:389
  7.5 5.2 %copy-start = (f32[1,64,512]{2,1,0:T(8,128)S(1)}, f32[1,64,512]{2,1,0:T(8,128)}, u32[]{:S(2)}) copy-start(f32[1,64,512]{2,1,0:T(8,128)} %param.8) | copy-start | bytes 393220
  13.4 13.0 %collective-permute-start.2 = (f32[64,512]{1,0:T(8,128)S(1)}, f32[64,512]{1,0:T(8,128)S(1)}, u32[]{:S(2)}, u32[]{:S(2)}) collective-permute-start(f32[64,512]{1,0:T(8,128)S(1)} %get-tuple-element.36.near_ref), channel_id=1, source_target_pairs={{0,1},{1,0},{2,3},{3,2},{4,5},{5,4},{6,7},{7,6},{8,9},{9,8},{10,11... | collective-permute-start | bytes 393224 | tf_op jit(solution)/shard_map/ppermute | solution.py:428
  13.5 12.9 %collective-permute-start.3 = (f32[64,512]{1,0:T(8,128)S(1)}, f32[64,512]{1,0:T(8,128)S(1)}, u32[]{:S(2)}, u32[]{:S(2)}) collective-permute-start(f32[64,512]{1,0:T(8,128)S(1)} %get-tuple-element.37.far_ref), channel_id=1, source_target_pairs={{0,31},{1,2},{2,1},{3,4},{4,3},{5,6},{6,5},{7,8},{8,7},{9,10},{10,... | collective-permute-start | bytes 393224 | tf_op jit(solution)/shard_map/ppermute | solution.py:426
  28.0 13.6 %collective-permute-start.4 = (f32[64,512]{1,0:T(8,128)S(1)}, f32[64,512]{1,0:T(8,128)S(1)}, u32[]{:S(2)}, u32[]{:S(2)}) collective-permute-start(f32[64,512]{1,0:T(8,128)S(1)} %get-tuple-element.42.near_ref), channel_id=1, source_target_pairs={{0,1},{1,0},{2,3},{3,2},{4,5},{5,4},{6,7},{7,6},{8,9},{9,8},{10,11... | collective-permute-start | bytes 393224 | tf_op jit(solution)/shard_map/ppermute | solution.py:428
  28.8 12.8 %collective-permute-start.5 = (f32[64,512]{1,0:T(8,128)S(1)}, f32[64,512]{1,0:T(8,128)S(1)}, u32[]{:S(2)}, u32[]{:S(2)}) collective-permute-start(f32[64,512]{1,0:T(8,128)S(1)} %get-tuple-element.43.far_ref), channel_id=1, source_target_pairs={{0,31},{1,2},{2,1},{3,4},{4,3},{5,6},{6,5},{7,8},{8,7},{9,10},{10,... | collective-permute-start | bytes 393224 | tf_op jit(solution)/shard_map/ppermute | solution.py:426
  43.0 10.1 %collective-permute-start.6 = (f32[64,512]{1,0:T(8,128)S(1)}, f32[64,512]{1,0:T(8,128)S(1)}, u32[]{:S(2)}, u32[]{:S(2)}) collective-permute-start(f32[64,512]{1,0:T(8,128)S(1)} %get-tuple-element.49), channel_id=1, source_target_pairs={{1,0},{2,1},{3,2},{4,3},{5,4},{6,5},{7,6},{8,7},{9,8},{10,9},{11,1... | collective-permute-start | bytes 393224 | tf_op jit(solution)/shard_map/ppermute | solution.py:426

commit v6 on v5

--- a/solution.py
+++ b/solution.py
@@ -161,7 +161,8 @@
     lines = jnp.concatenate([coef[p * used : (p + 1) * used, :] for p in range(per_row)], axis=1)
     slots = pay_ref.shape[0]
     pay_ref[:, :used, :] = jnp.broadcast_to(lines[None], (slots, used, LANES))
-    pay_ref[:, used : used + 1, :] = jnp.broadcast_to(gram_row[None], (slots, 1, LANES))
+    if gram_row is not None:
+        pay_ref[:, used : used + 1, :] = jnp.broadcast_to(gram_row[None], (slots, 1, LANES))
 
 
 def second_kernel(
@@ -312,8 +313,7 @@
     def block(n):
         return y[n] + block_product(both, high_ref, low_ref, start, n)
 
-    no_gram = jnp.zeros((1, LANES), F32)
-    finish(block, terms, even if pairs else None, load_ref, pieces, no_gram, near_out, far_out, pay_ref)
+    finish(block, terms, even if pairs else None, load_ref, pieces, None, near_out, far_out, pay_ref)
 
 
 def last_kernel(
@@ -430,7 +430,7 @@
         first = step == 0
         if step < ITERS - 1:
             inputs = [gathered, near, far, near_in, far_in, mult, masks, pieces, load[0], high, low]
-            outputs = [half, half, payload, full, full]
+            outputs = [half, half, ((devices, slot - 1, LANES), F32), full, full]
             if first:
                 outputs.append(rows)
             else:

time: 54.4 us -> 54.4 us (level)
  no operation moved by 1% of the time
where the time goes in v6:
time: 54.4 us; the launch traced here: 54.2 us
  blocking collectives  32.5 us (60%)
  starting transfers between devices  8.84 us (16%)
  Pallas kernels  8 us (15%)
  waiting for transfers between devices  2.87 us (5%)
  between operations  2.02 us (4%)
    all_to_all x3, blocking collectives, shards(): gathered = lax.all_to_all(pay_out, AXES, 0, 0)  32.5 us
    ppermute x3, starting transfers between devices, shards(): far_in = lax.ppermute(far, AXES, far_pairs if step < ITERS - 1 else back)  3.29 us
    ppermute x1, starting transfers between devices, shards(): halo = lax.ppermute(warm_start[0], AXES, ring)  3.02 us
    pallas_call x2, Pallas kernels, shards(): pl.pallas_call(functools.partial(middle_kernel, terms, first, step < ITER...  2.92 us
    ppermute x1, waiting for transfers between devices, shards(): halo_tail = lax.ppermute(tail, AXES, ring)  2.85 us
    pallas_call x1, Pallas kernels, shards(): pl.pallas_call(functools.partial(first_kernel, terms), out_shape=shaped((...  2.35 us
    ppermute x1, starting transfers between devices, shards(): halo_tail = lax.ppermute(tail, AXES, ring)  1.61 us
  transfers between devices with their start and end apart: 7, of which 1 were waited for; matrix products, arithmetic and copies ran while one was open for 0% of the time, Pallas kernels for 6%

profile of v6, /device:TPU:0, one launch (start us, length us, event | category | flops | bytes accessed | tf_op | source)
XLA Modules:
  0.0 54.2 jit_solution(10054681818899415396)
XLA Ops:
  0.6 3.0 %collective-permute-start = (f32[64,512]{1,0:T(8,128)}, f32[64,512]{1,0:T(8,128)S(1)}, u32[]{:S(2)}, u32[]{:S(2)}) collective-permute-start(f32[64,512]{1,0:T(8,128)} %bitcast.11), channel_id=1, source_target_pairs={{0,1},{1,2},{2,3},{3,4},{4,5},{5,6},{6,7},{7,8},{8,9},{9,10},{10,1... | collective-permute-start | bytes 393224 | tf_op jit(solution)/shard_map/ppermute | solution.py:375
  5.0 0.9 %pack.1 = (f32[64,512]{1,0:T(8,128)S(1)}, f32[8,512]{1,0:T(8,128)S(1)}) custom-call(s32[1]{0:T(128)S(6)} %copy.9.count_ref, s32[1]{0:T(128)S(6)} %copy.10.from_ref, f32[64,512]{1,0:T(8,128)} %bitcast.12, f32[6,1,512]{2,1,0:T(1,128)} %bitcast.13), custom_call_target="tpu_custom_call" | custom-call | tf_op jit(solution)/shard_map/pack/pallas_call | solution.py:376
  5.9 1.6 %collective-permute-start.1 = (f32[8,512]{1,0:T(8,128)S(1)}, f32[8,512]{1,0:T(8,128)S(1)}, u32[]{:S(2)}, u32[]{:S(2)}) collective-permute-start(f32[8,512]{1,0:T(8,128)S(1)} %get-tuple-element.30.tail_ref), channel_id=1, source_target_pairs={{0,1},{1,2},{2,3},{3,4},{4,5},{5,6},{6,7},{7,8},{8,9},{9,10},{10,1... | collective-permute-start | bytes 49160 | tf_op jit(solution)/shard_map/ppermute | solution.py:389
  7.5 0.0 copy-start
  7.5 2.4 %first.1 = (bf16[8,1024,128]{2,1,0:T(8,128)(2,1)S(1)}, bf16[8,1024,128]{2,1,0:T(8,128)(2,1)S(1)}, f32[64,1024]{1,0:T(8,128)S(1)}, f32[1,128]{1,0:T(1,128)S(1)}) custom-call(f32[1024,1024]{1,0:T(8,128)} %bitcast.10, f32[64,512]{1,0:T(8,128)S(1)} %get-tuple-element.29.msg_ref, f32[8,512]{1,0:T(8,128)S(1)} %get-tuple-element.30.tail_ref), custom_call_target="tpu_custom_call" | custom-call | flops 268435456 | bytes 8388608 | tf_op jit(solution)/shard_map/first/pallas_call | solution.py:390
  9.9 2.8 %collective-permute-done.1.halo_tail_ref = f32[8,512]{1,0:T(8,128)S(1)} collective-permute-done((f32[8,512]{1,0:T(8,128)S(1)}, f32[8,512]{1,0:T(8,128)S(1)}, u32[]{:S(2)}, u32[]{:S(2)}) %collective-permute-start.1) | collective-permute-done | bytes 16416 | tf_op jit(solution)/shard_map/ppermute | solution.py:389
  12.7 0.0 collective-permute-done.halo_ref
  12.7 0.0 copy-done
  12.7 0.7 %second.1 = (f32[64,512]{1,0:T(8,128)S(1)}, f32[64,512]{1,0:T(8,128)S(1)}, f32[32,4,128]{2,1,0:T(4,128)S(1)}, f32[64,1024]{1,0:T(8,128)S(1)}, f32[2,1024]{1,0:T(2,128)S(1)}, /*index=5*/bf16[24,1024]{1,0:T(8,128)(2,1)S(1)}) custom-call(bf16[8,1024,128]{2,1,0:T(8,128)(2,1)S(1)} %get-tuple-element.31.high_ref, ...), custom_call_target="tpu_custom_call" | custom-call | tf_op jit(solution)/shard_map/second/pallas_call | solution.py:414
  13.4 0.1 collective-permute-start.2
  13.5 1.6 %collective-permute-start.3 = (f32[64,512]{1,0:T(8,128)S(1)}, f32[64,512]{1,0:T(8,128)S(1)}, u32[]{:S(2)}, u32[]{:S(2)}) collective-permute-start(f32[64,512]{1,0:T(8,128)S(1)} %get-tuple-element.37.far_ref), channel_id=1, source_target_pairs={{0,31},{1,2},{2,1},{3,4},{4,3},{5,6},{6,5},{7,8},{8,7},{9,10},{10,... | collective-permute-start | bytes 393224 | tf_op jit(solution)/shard_map/ppermute | solution.py:426
  15.1 11.3 %all_to_all.15.sum_ref = f32[32,4,128]{2,1,0:T(4,128)S(1)} all-to-all(f32[32,4,128]{2,1,0:T(4,128)S(1)} %get-tuple-element.35), channel_id=1, replica_groups=mesh['group'=4,'dev'=8] {'group','dev'}, dimensions={0} | all-to-all | bytes 131072 | tf_op jit(solution)/shard_map/all_to_all | solution.py:429
  26.4 0.0 collective-permute-done.2.near_in
  26.4 0.0 collective-permute-done.3.far_in
  26.4 1.5 %shard_map.85 = (f32[64,512]{1,0:T(8,128)S(1)}, f32[64,512]{1,0:T(8,128)S(1)}, f32[32,3,128]{2,1,0:T(4,128)S(1)}, f32[64,1024]{1,0:T(8,128)S(1)}, f32[64,1024]{1,0:T(8,128)S(1)}, /*index=5*/f32[24,128]{1,0:T(8,128)S(1)}) custom-call(f32[32,4,128]{2,1,0:T(4,128)S(1)} %all_to_all.15.sum_ref, f32[64,512]{1,0:T(8,128)S(1)} %get-tuple-element.36.near_ref, ...), custom_call_target="tpu_custom_call" | custom-call | tf_op jit(solution)/shard_map/pallas_call | solution.py:438
  28.0 0.8 %collective-permute-start.4 = (f32[64,512]{1,0:T(8,128)S(1)}, f32[64,512]{1,0:T(8,128)S(1)}, u32[]{:S(2)}, u32[]{:S(2)}) collective-permute-start(f32[64,512]{1,0:T(8,128)S(1)} %get-tuple-element.42.near_ref), channel_id=1, source_target_pairs={{0,1},{1,0},{2,3},{3,2},{4,5},{5,4},{6,7},{7,6},{8,9},{9,8},{10,11... | collective-permute-start | bytes 393224 | tf_op jit(solution)/shard_map/ppermute | solution.py:428
  28.8 0.9 %collective-permute-start.5 = (f32[64,512]{1,0:T(8,128)S(1)}, f32[64,512]{1,0:T(8,128)S(1)}, u32[]{:S(2)}, u32[]{:S(2)}) collective-permute-start(f32[64,512]{1,0:T(8,128)S(1)} %get-tuple-element.43.far_ref), channel_id=1, source_target_pairs={{0,31},{1,2},{2,1},{3,4},{4,3},{5,6},{6,5},{7,8},{8,7},{9,10},{10,... | collective-permute-start | bytes 393224 | tf_op jit(solution)/shard_map/ppermute | solution.py:426
  29.7 11.9 %all_to_all.16.sum_ref = f32[32,3,128]{2,1,0:T(4,128)S(1)} all-to-all(f32[32,3,128]{2,1,0:T(4,128)S(1)} %get-tuple-element.41), channel_id=1, replica_groups=mesh['group'=4,'dev'=8] {'group','dev'}, dimensions={0} | all-to-all | bytes 98304 | tf_op jit(solution)/shard_map/all_to_all | solution.py:429
  41.6 0.0 collective-permute-done.4.near_in
  41.6 0.0 collective-permute-done.5.far_in
  41.6 1.4 %shard_map.86 = (f32[64,512]{1,0:T(8,128)S(1)}, f32[64,512]{1,0:T(8,128)S(1)}, f32[32,3,128]{2,1,0:T(4,128)S(1)}, f32[64,1024]{1,0:T(8,128)S(1)}, f32[64,1024]{1,0:T(8,128)S(1)}) custom-call(f32[32,3,128]{2,1,0:T(4,128)S(1)} %all_to_all.16.sum_ref, f32[64,512]{1,0:T(8,128)S(1)} %get-tuple-element.42.near_ref, f32[64,512]{1,0:T(8,128)S(1)} %get-tuple-element.43.far_ref, ...), custom_call_target="tpu_custom_call" | custom-call | tf_op jit(solution)/shard_map/pallas_call | solution.py:438
  43.0 0.8 %collective-permute-start.6 = (f32[64,512]{1,0:T(8,128)S(1)}, f32[64,512]{1,0:T(8,128)S(1)}, u32[]{:S(2)}, u32[]{:S(2)}) collective-permute-start(f32[64,512]{1,0:T(8,128)S(1)} %get-tuple-element.49), channel_id=1, source_target_pairs={{1,0},{2,1},{3,2},{4,3},{5,4},{6,5},{7,6},{8,7},{9,8},{10,9},{11,1... | collective-permute-start | bytes 393224 | tf_op jit(solution)/shard_map/ppermute | solution.py:426
  43.8 9.3 %all_to_all.17.sum_ref = f32[32,3,128]{2,1,0:T(4,128)S(1)} all-to-all(f32[32,3,128]{2,1,0:T(4,128)S(1)} %get-tuple-element.47), channel_id=1, replica_groups=mesh['group'=4,'dev'=8] {'group','dev'}, dimensions={0} | all-to-all | bytes 98304 | tf_op jit(solution)/shard_map/all_to_all | solution.py:429
  53.1 0.0 collective-permute-done.6.next_in
  53.1 1.1 %last.1 = (f32[64,512]{1,0:T(8,128)}, f32[64,512]{1,0:T(8,128)}, f32[6,64]{1,0:T(8,128)}) custom-call(f32[32,3,128]{2,1,0:T(4,128)S(1)} %all_to_all.17.sum_ref, f32[64,512]{1,0:T(8,128)S(1)} %get-tuple-element.48.own_ref, f32[64,512]{1,0:T(8,128)S(1)} %collective-permute-done.6.next_in, f32[64,1024]{1,0:T(8,128)S(1)} %get-tuple-element.50.mult_ref, ...), custom_call_target="tpu_custom_call" | custom-call | tf_op jit(solution)/shard_map/last/pallas_call | solution.py:451
Async XLA Ops:
  0.6 12.1 %collective-permute-start = (f32[64,512]{1,0:T(8,128)}, f32[64,512]{1,0:T(8,128)S(1)}, u32[]{:S(2)}, u32[]{:S(2)}) collective-permute-start(f32[64,512]{1,0:T(8,128)} %bitcast.11), channel_id=1, source_target_pairs={{0,1},{1,2},{2,3},{3,4},{4,5},{5,6},{6,7},{7,8},{8,9},{9,10},{10,1... | collective-permute-start | bytes 393224 | tf_op jit(solution)/shard_map/ppermute | solution.py:375
  5.9 6.8 %collective-permute-start.1 = (f32[8,512]{1,0:T(8,128)S(1)}, f32[8,512]{1,0:T(8,128)S(1)}, u32[]{:S(2)}, u32[]{:S(2)}) collective-permute-start(f32[8,512]{1,0:T(8,128)S(1)} %get-tuple-element.30.tail_ref), channel_id=1, source_target_pairs={{0,1},{1,2},{2,3},{3,4},{4,5},{5,6},{6,7},{7,8},{8,9},{9,10},{10,1... | collective-permute-start | bytes 49160 | tf_op jit(solution)/shard_map/ppermute | solution.py:389
  7.5 5.2 %copy-start = (f32[1,64,512]{2,1,0:T(8,128)S(1)}, f32[1,64,512]{2,1,0:T(8,128)}, u32[]{:S(2)}) copy-start(f32[1,64,512]{2,1,0:T(8,128)} %param.8) | copy-start | bytes 393220
  13.4 13.0 %collective-permute-start.2 = (f32[64,512]{1,0:T(8,128)S(1)}, f32[64,512]{1,0:T(8,128)S(1)}, u32[]{:S(2)}, u32[]{:S(2)}) collective-permute-start(f32[64,512]{1,0:T(8,128)S(1)} %get-tuple-element.36.near_ref), channel_id=1, source_target_pairs={{0,1},{1,0},{2,3},{3,2},{4,5},{5,4},{6,7},{7,6},{8,9},{9,8},{10,11... | collective-permute-start | bytes 393224 | tf_op jit(solution)/shard_map/ppermute | solution.py:428
  13.5 12.9 %collective-permute-start.3 = (f32[64,512]{1,0:T(8,128)S(1)}, f32[64,512]{1,0:T(8,128)S(1)}, u32[]{:S(2)}, u32[]{:S(2)}) collective-permute-start(f32[64,512]{1,0:T(8,128)S(1)} %get-tuple-element.37.far_ref), channel_id=1, source_target_pairs={{0,31},{1,2},{2,1},{3,4},{4,3},{5,6},{6,5},{7,8},{8,7},{9,10},{10,... | collective-permute-start | bytes 393224 | tf_op jit(solution)/shard_map/ppermute | solution.py:426
  28.0 13.6 %collective-permute-start.4 = (f32[64,512]{1,0:T(8,128)S(1)}, f32[64,512]{1,0:T(8,128)S(1)}, u32[]{:S(2)}, u32[]{:S(2)}) collective-permute-start(f32[64,512]{1,0:T(8,128)S(1)} %get-tuple-element.42.near_ref), channel_id=1, source_target_pairs={{0,1},{1,0},{2,3},{3,2},{4,5},{5,4},{6,7},{7,6},{8,9},{9,8},{10,11... | collective-permute-start | bytes 393224 | tf_op jit(solution)/shard_map/ppermute | solution.py:428
  28.8 12.8 %collective-permute-start.5 = (f32[64,512]{1,0:T(8,128)S(1)}, f32[64,512]{1,0:T(8,128)S(1)}, u32[]{:S(2)}, u32[]{:S(2)}) collective-permute-start(f32[64,512]{1,0:T(8,128)S(1)} %get-tuple-element.43.far_ref), channel_id=1, source_target_pairs={{0,31},{1,2},{2,1},{3,4},{4,3},{5,6},{6,5},{7,8},{8,7},{9,10},{10,... | collective-permute-start | bytes 393224 | tf_op jit(solution)/shard_map/ppermute | solution.py:426
  43.0 10.1 %collective-permute-start.6 = (f32[64,512]{1,0:T(8,128)S(1)}, f32[64,512]{1,0:T(8,128)S(1)}, u32[]{:S(2)}, u32[]{:S(2)}) collective-permute-start(f32[64,512]{1,0:T(8,128)S(1)} %get-tuple-element.49), channel_id=1, source_target_pairs={{1,0},{2,1},{3,2},{4,3},{5,4},{6,5},{7,6},{8,7},{9,8},{10,9},{11,1... | collective-permute-start | bytes 393224 | tf_op jit(solution)/shard_map/ppermute | solution.py:426

commit v7 on v5

--- a/solution.py
+++ b/solution.py
@@ -304,13 +304,11 @@
         mult = jnp.where(mask_ref[1:2, lanes] > 0.0, jnp.maximum(mult, 0.0), mult)
         mult_out[:, lanes] = mult
         upd_out[:, lanes] = update
-        both = jnp.concatenate(split(-mult if start < width else mult), axis=0)
-        if start + DEPTH < 2 * width:
-            parts = [block_product(both, high_ref, low_ref, start, n) for n in range(2 * width // WIDE)]
-            y = [a + b for a, b in zip(y, parts)] if y else parts
+        y.append(jnp.concatenate(split(-mult if start < width else mult), axis=0))
+    both = jnp.concatenate(y, axis=1)
 
     def block(n):
-        return y[n] + block_product(both, high_ref, low_ref, start, n)
+        return block_product(both, high_ref, low_ref, 0, n)
 
     no_gram = jnp.zeros((1, LANES), F32)
     finish(block, terms, even if pairs else None, load_ref, pieces, no_gram, near_out, far_out, pay_ref)

time: 54.4 us -> 54.4 us (level)
  no operation moved by 1% of the time
where the time goes in v7:
time: 54.4 us; the launch traced here: 54.2 us
  blocking collectives  32.5 us (60%)
  starting transfers between devices  8.85 us (16%)
  Pallas kernels  7.96 us (15%)
  waiting for transfers between devices  2.87 us (5%)
  between operations  2.02 us (4%)
    all_to_all x3, blocking collectives, shards(): gathered = lax.all_to_all(pay_out, AXES, 0, 0)  32.5 us
    ppermute x3, starting transfers between devices, shards(): far_in = lax.ppermute(far, AXES, far_pairs if step < ITERS - 1 else back)  3.3 us
    ppermute x1, starting transfers between devices, shards(): halo = lax.ppermute(warm_start[0], AXES, ring)  3.02 us
    pallas_call x2, Pallas kernels, shards(): pl.pallas_call(functools.partial(middle_kernel, terms, first, step < ITER...  2.89 us
    ppermute x1, waiting for transfers between devices, shards(): halo_tail = lax.ppermute(tail, AXES, ring)  2.85 us
    pallas_call x1, Pallas kernels, shards(): pl.pallas_call(functools.partial(first_kernel, terms), out_shape=shaped((...  2.35 us
    ppermute x1, starting transfers between devices, shards(): halo_tail = lax.ppermute(tail, AXES, ring)  1.61 us
  transfers between devices with their start and end apart: 7, of which 1 were waited for; matrix products, arithmetic and copies ran while one was open for 0% of the time, Pallas kernels for 6%

profile of v7, /device:TPU:0, one launch (start us, length us, event | category | flops | bytes accessed | tf_op | source)
XLA Modules:
  0.0 54.2 jit_solution(1220082088385060780)
XLA Ops:
  0.6 3.0 %collective-permute-start = (f32[64,512]{1,0:T(8,128)}, f32[64,512]{1,0:T(8,128)S(1)}, u32[]{:S(2)}, u32[]{:S(2)}) collective-permute-start(f32[64,512]{1,0:T(8,128)} %bitcast.11), channel_id=1, source_target_pairs={{0,1},{1,2},{2,3},{3,4},{4,5},{5,6},{6,7},{7,8},{8,9},{9,10},{10,1... | collective-permute-start | bytes 393224 | tf_op jit(solution)/shard_map/ppermute | solution.py:373
  5.0 0.9 %pack.1 = (f32[64,512]{1,0:T(8,128)S(1)}, f32[8,512]{1,0:T(8,128)S(1)}) custom-call(s32[1]{0:T(128)S(6)} %copy.9.count_ref, s32[1]{0:T(128)S(6)} %copy.10.from_ref, f32[64,512]{1,0:T(8,128)} %bitcast.12, f32[6,1,512]{2,1,0:T(1,128)} %bitcast.13), custom_call_target="tpu_custom_call" | custom-call | tf_op jit(solution)/shard_map/pack/pallas_call | solution.py:374
  5.9 1.6 %collective-permute-start.1 = (f32[8,512]{1,0:T(8,128)S(1)}, f32[8,512]{1,0:T(8,128)S(1)}, u32[]{:S(2)}, u32[]{:S(2)}) collective-permute-start(f32[8,512]{1,0:T(8,128)S(1)} %get-tuple-element.30.tail_ref), channel_id=1, source_target_pairs={{0,1},{1,2},{2,3},{3,4},{4,5},{5,6},{6,7},{7,8},{8,9},{9,10},{10,1... | collective-permute-start | bytes 49160 | tf_op jit(solution)/shard_map/ppermute | solution.py:387
  7.5 0.0 copy-start
  7.5 2.4 %first.1 = (bf16[8,1024,128]{2,1,0:T(8,128)(2,1)S(1)}, bf16[8,1024,128]{2,1,0:T(8,128)(2,1)S(1)}, f32[64,1024]{1,0:T(8,128)S(1)}, f32[1,128]{1,0:T(1,128)S(1)}) custom-call(f32[1024,1024]{1,0:T(8,128)} %bitcast.10, f32[64,512]{1,0:T(8,128)S(1)} %get-tuple-element.29.msg_ref, f32[8,512]{1,0:T(8,128)S(1)} %get-tuple-element.30.tail_ref), custom_call_target="tpu_custom_call" | custom-call | flops 268435456 | bytes 8388608 | tf_op jit(solution)/shard_map/first/pallas_call | solution.py:388
  9.9 2.8 %collective-permute-done.1.halo_tail_ref = f32[8,512]{1,0:T(8,128)S(1)} collective-permute-done((f32[8,512]{1,0:T(8,128)S(1)}, f32[8,512]{1,0:T(8,128)S(1)}, u32[]{:S(2)}, u32[]{:S(2)}) %collective-permute-start.1) | collective-permute-done | bytes 16416 | tf_op jit(solution)/shard_map/ppermute | solution.py:387
  12.7 0.0 collective-permute-done.halo_ref
  12.7 0.0 copy-done
  12.7 0.7 %second.1 = (f32[64,512]{1,0:T(8,128)S(1)}, f32[64,512]{1,0:T(8,128)S(1)}, f32[32,4,128]{2,1,0:T(4,128)S(1)}, f32[64,1024]{1,0:T(8,128)S(1)}, f32[2,1024]{1,0:T(2,128)S(1)}, /*index=5*/bf16[24,1024]{1,0:T(8,128)(2,1)S(1)}) custom-call(bf16[8,1024,128]{2,1,0:T(8,128)(2,1)S(1)} %get-tuple-element.31.high_ref, ...), custom_call_target="tpu_custom_call" | custom-call | tf_op jit(solution)/shard_map/second/pallas_call | solution.py:412
  13.4 0.1 collective-permute-start.2
  13.5 1.6 %collective-permute-start.3 = (f32[64,512]{1,0:T(8,128)S(1)}, f32[64,512]{1,0:T(8,128)S(1)}, u32[]{:S(2)}, u32[]{:S(2)}) collective-permute-start(f32[64,512]{1,0:T(8,128)S(1)} %get-tuple-element.37.far_ref), channel_id=1, source_target_pairs={{0,31},{1,2},{2,1},{3,4},{4,3},{5,6},{6,5},{7,8},{8,7},{9,10},{10,... | collective-permute-start | bytes 393224 | tf_op jit(solution)/shard_map/ppermute | solution.py:424
  15.1 11.3 %all_to_all.15.sum_ref = f32[32,4,128]{2,1,0:T(4,128)S(1)} all-to-all(f32[32,4,128]{2,1,0:T(4,128)S(1)} %get-tuple-element.35), channel_id=1, replica_groups=mesh['group'=4,'dev'=8] {'group','dev'}, dimensions={0} | all-to-all | bytes 131072 | tf_op jit(solution)/shard_map/all_to_all | solution.py:427
  26.4 0.0 collective-permute-done.2.near_in
  26.4 0.0 collective-permute-done.3.far_in
  26.4 1.5 %shard_map.85 = (f32[64,512]{1,0:T(8,128)S(1)}, f32[64,512]{1,0:T(8,128)S(1)}, f32[32,4,128]{2,1,0:T(4,128)S(1)}, f32[64,1024]{1,0:T(8,128)S(1)}, f32[64,1024]{1,0:T(8,128)S(1)}, /*index=5*/f32[24,128]{1,0:T(8,128)S(1)}) custom-call(f32[32,4,128]{2,1,0:T(4,128)S(1)} %all_to_all.15.sum_ref, f32[64,512]{1,0:T(8,128)S(1)} %get-tuple-element.36.near_ref, ...), custom_call_target="tpu_custom_call" | custom-call | tf_op jit(solution)/shard_map/pallas_call | solution.py:436
  27.9 0.9 %collective-permute-start.4 = (f32[64,512]{1,0:T(8,128)S(1)}, f32[64,512]{1,0:T(8,128)S(1)}, u32[]{:S(2)}, u32[]{:S(2)}) collective-permute-start(f32[64,512]{1,0:T(8,128)S(1)} %get-tuple-element.42.near_ref), channel_id=1, source_target_pairs={{0,1},{1,0},{2,3},{3,2},{4,5},{5,4},{6,7},{7,6},{8,9},{9,8},{10,11... | collective-permute-start | bytes 393224 | tf_op jit(solution)/shard_map/ppermute | solution.py:426
  28.8 0.9 %collective-permute-start.5 = (f32[64,512]{1,0:T(8,128)S(1)}, f32[64,512]{1,0:T(8,128)S(1)}, u32[]{:S(2)}, u32[]{:S(2)}) collective-permute-start(f32[64,512]{1,0:T(8,128)S(1)} %get-tuple-element.43.far_ref), channel_id=1, source_target_pairs={{0,31},{1,2},{2,1},{3,4},{4,3},{5,6},{6,5},{7,8},{8,7},{9,10},{10,... | collective-permute-start | bytes 393224 | tf_op jit(solution)/shard_map/ppermute | solution.py:424
  29.7 11.9 %all_to_all.16.sum_ref = f32[32,4,128]{2,1,0:T(4,128)S(1)} all-to-all(f32[32,4,128]{2,1,0:T(4,128)S(1)} %get-tuple-element.41), channel_id=1, replica_groups=mesh['group'=4,'dev'=8] {'group','dev'}, dimensions={0} | all-to-all | bytes 131072 | tf_op jit(solution)/shard_map/all_to_all | solution.py:427
  41.6 0.0 collective-permute-done.4.near_in
  41.6 0.0 collective-permute-done.5.far_in
  41.6 1.4 %shard_map.86 = (f32[64,512]{1,0:T(8,128)S(1)}, f32[64,512]{1,0:T(8,128)S(1)}, f32[32,4,128]{2,1,0:T(4,128)S(1)}, f32[64,1024]{1,0:T(8,128)S(1)}, f32[64,1024]{1,0:T(8,128)S(1)}) custom-call(f32[32,4,128]{2,1,0:T(4,128)S(1)} %all_to_all.16.sum_ref, f32[64,512]{1,0:T(8,128)S(1)} %get-tuple-element.42.near_ref, f32[64,512]{1,0:T(8,128)S(1)} %get-tuple-element.43.far_ref, ...), custom_call_target="tpu_custom_call" | custom-call | tf_op jit(solution)/shard_map/pallas_call | solution.py:436
  43.0 0.8 %collective-permute-start.6 = (f32[64,512]{1,0:T(8,128)S(1)}, f32[64,512]{1,0:T(8,128)S(1)}, u32[]{:S(2)}, u32[]{:S(2)}) collective-permute-start(f32[64,512]{1,0:T(8,128)S(1)} %get-tuple-element.49), channel_id=1, source_target_pairs={{1,0},{2,1},{3,2},{4,3},{5,4},{6,5},{7,6},{8,7},{9,8},{10,9},{11,1... | collective-permute-start | bytes 393224 | tf_op jit(solution)/shard_map/ppermute | solution.py:424
  43.8 9.3 %all_to_all.17.sum_ref = f32[32,4,128]{2,1,0:T(4,128)S(1)} all-to-all(f32[32,4,128]{2,1,0:T(4,128)S(1)} %get-tuple-element.47), channel_id=1, replica_groups=mesh['group'=4,'dev'=8] {'group','dev'}, dimensions={0} | all-to-all | bytes 131072 | tf_op jit(solution)/shard_map/all_to_all | solution.py:427
  53.1 0.0 collective-permute-done.6.next_in
  53.1 1.1 %last.1 = (f32[64,512]{1,0:T(8,128)}, f32[64,512]{1,0:T(8,128)}, f32[6,64]{1,0:T(8,128)}) custom-call(f32[32,4,128]{2,1,0:T(4,128)S(1)} %all_to_all.17.sum_ref, f32[64,512]{1,0:T(8,128)S(1)} %get-tuple-element.48.own_ref, f32[64,512]{1,0:T(8,128)S(1)} %collective-permute-done.6.next_in, f32[64,1024]{1,0:T(8,128)S(1)} %get-tuple-element.50.mult_ref, ...), custom_call_target="tpu_custom_call" | custom-call | tf_op jit(solution)/shard_map/last/pallas_call | solution.py:449
Async XLA Ops:
  0.6 12.1 %collective-permute-start = (f32[64,512]{1,0:T(8,128)}, f32[64,512]{1,0:T(8,128)S(1)}, u32[]{:S(2)}, u32[]{:S(2)}) collective-permute-start(f32[64,512]{1,0:T(8,128)} %bitcast.11), channel_id=1, source_target_pairs={{0,1},{1,2},{2,3},{3,4},{4,5},{5,6},{6,7},{7,8},{8,9},{9,10},{10,1... | collective-permute-start | bytes 393224 | tf_op jit(solution)/shard_map/ppermute | solution.py:373
  5.9 6.8 %collective-permute-start.1 = (f32[8,512]{1,0:T(8,128)S(1)}, f32[8,512]{1,0:T(8,128)S(1)}, u32[]{:S(2)}, u32[]{:S(2)}) collective-permute-start(f32[8,512]{1,0:T(8,128)S(1)} %get-tuple-element.30.tail_ref), channel_id=1, source_target_pairs={{0,1},{1,2},{2,3},{3,4},{4,5},{5,6},{6,7},{7,8},{8,9},{9,10},{10,1... | collective-permute-start | bytes 49160 | tf_op jit(solution)/shard_map/ppermute | solution.py:387
  7.5 5.2 %copy-start = (f32[1,64,512]{2,1,0:T(8,128)S(1)}, f32[1,64,512]{2,1,0:T(8,128)}, u32[]{:S(2)}) copy-start(f32[1,64,512]{2,1,0:T(8,128)} %param.8) | copy-start | bytes 393220
  13.4 13.0 %collective-permute-start.2 = (f32[64,512]{1,0:T(8,128)S(1)}, f32[64,512]{1,0:T(8,128)S(1)}, u32[]{:S(2)}, u32[]{:S(2)}) collective-permute-start(f32[64,512]{1,0:T(8,128)S(1)} %get-tuple-element.36.near_ref), channel_id=1, source_target_pairs={{0,1},{1,0},{2,3},{3,2},{4,5},{5,4},{6,7},{7,6},{8,9},{9,8},{10,11... | collective-permute-start | bytes 393224 | tf_op jit(solution)/shard_map/ppermute | solution.py:426
  13.5 12.9 %collective-permute-start.3 = (f32[64,512]{1,0:T(8,128)S(1)}, f32[64,512]{1,0:T(8,128)S(1)}, u32[]{:S(2)}, u32[]{:S(2)}) collective-permute-start(f32[64,512]{1,0:T(8,128)S(1)} %get-tuple-element.37.far_ref), channel_id=1, source_target_pairs={{0,31},{1,2},{2,1},{3,4},{4,3},{5,6},{6,5},{7,8},{8,7},{9,10},{10,... | collective-permute-start | bytes 393224 | tf_op jit(solution)/shard_map/ppermute | solution.py:424
  27.9 13.6 %collective-permute-start.4 = (f32[64,512]{1,0:T(8,128)S(1)}, f32[64,512]{1,0:T(8,128)S(1)}, u32[]{:S(2)}, u32[]{:S(2)}) collective-permute-start(f32[64,512]{1,0:T(8,128)S(1)} %get-tuple-element.42.near_ref), channel_id=1, source_target_pairs={{0,1},{1,0},{2,3},{3,2},{4,5},{5,4},{6,7},{7,6},{8,9},{9,8},{10,11... | collective-permute-start | bytes 393224 | tf_op jit(solution)/shard_map/ppermute | solution.py:426
  28.8 12.8 %collective-permute-start.5 = (f32[64,512]{1,0:T(8,128)S(1)}, f32[64,512]{1,0:T(8,128)S(1)}, u32[]{:S(2)}, u32[]{:S(2)}) collective-permute-start(f32[64,512]{1,0:T(8,128)S(1)} %get-tuple-element.43.far_ref), channel_id=1, source_target_pairs={{0,31},{1,2},{2,1},{3,4},{4,3},{5,6},{6,5},{7,8},{8,7},{9,10},{10,... | collective-permute-start | bytes 393224 | tf_op jit(solution)/shard_map/ppermute | solution.py:424
  43.0 10.1 %collective-permute-start.6 = (f32[64,512]{1,0:T(8,128)S(1)}, f32[64,512]{1,0:T(8,128)S(1)}, u32[]{:S(2)}, u32[]{:S(2)}) collective-permute-start(f32[64,512]{1,0:T(8,128)S(1)} %get-tuple-element.49), channel_id=1, source_target_pairs={{1,0},{2,1},{3,2},{4,3},{5,4},{6,5},{7,6},{8,7},{9,8},{10,9},{11,1... | collective-permute-start | bytes 393224 | tf_op jit(solution)/shard_map/ppermute | solution.py:424
